TPU v7x, 32 devices: a whole 2x2x4 slice. The times are simulated.
32 devices in a mesh: dp: 8 (over y, x, core), tensor: 4 (over z).
Axes of the slice: x: 2, y: 2, z: 4, core: 2. Of those that a mesh axis runs over, the one named last changes fastest.
Arguments:
- hidden: bfloat16 [8, 1280, 1120], P('dp', 'tensor'), may hold values from -6 to 6
- segment_ids: int32 [8, 1280], P('dp'), may hold values from 0 to 15, as said below
- lengths: int32 [8], P('dp'), may hold values from 640 to 1280, as said below
- norm1_gain: float32 [1120], replicated, may hold values from 0.25 to 1.75
- norm1_shift: float32 [1120], replicated, may hold values from -4 to 4
- qkv_weight: bfloat16 [3, 1120, 1120], P(None, None, 'tensor'), may hold values from -0.1875 to 0.1875
- qv_bias: float32 [2, 1120], P(None, 'tensor'), may hold values from -4 to 4
- out_weight: bfloat16 [1120, 1120], P('tensor'), may hold values from -1 to 1
- out_bias: float32 [1120], replicated, may hold values from -4 to 4
- norm2_gain: float32 [1120], replicated, may hold values from 0.25 to 1.75
- norm2_shift: float32 [1120], replicated, may hold values from -4 to 4
- up_weight: bfloat16 [1120, 4480], P(None, 'tensor'), may hold values from -0.1875 to 0.1875
- up_bias: float32 [4480], P('tensor'), may hold values from -4 to 4
- down_weight: bfloat16 [4480, 1120], P('tensor'), may hold values from -0.125 to 0.125
- down_bias: float32 [1120], replicated, may hold values from -4 to 4
- cotangent: bfloat16 [8, 1280, 1120], P('dp', 'tensor'), may hold values from -6 to 6
Outputs:
- output: bfloat16 [8, 1280, 1120], P('dp', 'tensor')
- input_grad: bfloat16 [8, 1280, 1120], P('dp', 'tensor')
- norm1_gain_grad: float32 [1120], replicated
- norm1_shift_grad: float32 [1120], replicated
- qkv_weight_grad: float32 [3, 1120, 1120], P(None, None, 'tensor')
- qv_bias_grad: float32 [2, 1120], P(None, 'tensor')
- out_weight_grad: float32 [1120, 1120], P('tensor')
- out_bias_grad: float32 [1120], replicated
- norm2_gain_grad: float32 [1120], replicated
- norm2_shift_grad: float32 [1120], replicated
- up_weight_grad: float32 [1120, 4480], P(None, 'tensor')
- up_bias_grad: float32 [4480], P('tensor')
- down_weight_grad: float32 [4480, 1120], P('tensor')
- down_bias_grad: float32 [1120], replicated
Inputs may be any that keep to these rules, and one draw needn't show every extreme that they name: `segment_ids`: along each row the ids start at 0 and never fall; a cell is a run of equal ids. `lengths`: some row is full and some row holds 640 live tokens.
All inputs are finite; a program needn't handle non-finite values.
Results may differ from a plain program's by a relative error of at most 0.012.
Values may be sent and summed in bfloat16 or wider, within the bound.
A program may use at most 256 MiB of HBM per device.

v0:
```python
import functools
import math

import jax
import jax.numpy as jnp
from jax import lax
from jax.experimental import pallas as pl
from jax.experimental.pallas import tpu as pltpu
from jax.sharding import PartitionSpec as P

HEAD = 56
EPS = 1e-05
LANES = 128
BLK = 256
BF = jnp.bfloat16
F32 = jnp.float32


def mm(a, b):
    return jnp.dot(a, b, preferred_element_type=F32)


def mm_nt(a, b):
    return lax.dot_general(a, b, (((1,), (1,)), ((), ())), preferred_element_type=F32)


def mm_tn(a, b):
    return lax.dot_general(a, b, (((0,), (0,)), ((), ())), preferred_element_type=F32)


def head_window(h):
    lo, hi = h * HEAD, (h + 1) * HEAD
    first = lo // LANES * LANES
    last = -(-hi // LANES) * LANES
    return first, last


def head_mask(h, rows):
    first, last = head_window(h)
    lane = lax.broadcasted_iota(jnp.int32, (rows, last - first), 1) + first
    return (lane >= h * HEAD) & (lane < (h + 1) * HEAD)


def stage_in(rank, src, dst, shard, width):
    wide = dst.shape[1]
    for s in range(src.shape[0] // shard):
        rel = pl.multiple_of((rank ^ s) * shard, 16)
        dst[s * shard : (s + 1) * shard, :width] = src[pl.ds(rel, shard), :]
    if wide > width:
        dst[:, width:] = jnp.zeros((dst.shape[0], wide - width), dst.dtype)


def project(rank, src, shard, width, products):
    @pl.loop(0, src.shape[0] // shard)
    def _(s):
        rel = pl.multiple_of((rank ^ s) * shard, 16)
        rows = pl.ds(pl.multiple_of(s * shard, 16), shard)
        x = src[pl.ds(rel, shard), :]
        for dst, weight, bias in products:
            value = dot_nt(x, weight[...])
            if bias is not None:
                value = value + bias
            dst[rows, :width] = value.astype(BF)

    for dst, _, _ in products:
        if dst.shape[1] > width:
            dst[:, width:] = jnp.zeros((dst.shape[0], dst.shape[1] - width), BF)


def stage_out(rank, src, dst, shard, width):
    for s in range(dst.shape[0] // shard):
        rel = pl.multiple_of((rank ^ s) * shard, 16)
        dst[pl.ds(rel, shard), :] = src[s * shard : (s + 1) * shard, :width]


def tile_mask(start_row, qb, kb):
    kpos = kb * BLK + lax.broadcasted_iota(jnp.int32, (BLK, BLK), 0)
    qpos = qb * BLK + lax.broadcasted_iota(jnp.int32, (BLK, BLK), 1)
    return (kpos <= qpos) & (kpos >= start_row)


def dot_nt(a, b):
    return lax.dot_general(a, b, (((1,), (1,)), ((), ())), preferred_element_type=F32)


def attn_fwd_kernel(heads, shard, meta, start, normed, wq, bias, out, lse, qs, ks, vs, vt, os, ot, ms, ls, acc):
    seq, width = out.shape
    scale2 = HEAD ** (-0.5) * math.log2(math.e)
    rank = meta[0]
    b_q, b_v = bias[0:1, :], bias[1:2, :]
    project(
        rank, normed, shard, width, [(qs, wq.at[0], b_q), (ks, wq.at[1], None), (vs, wq.at[2], b_v)]
    )
    blocks = seq // BLK

    @pl.loop(0, blocks)
    def _(b):
        rows = pl.ds(pl.multiple_of(b * BLK, BLK), BLK)
        flipped = vs[rows, :].astype(F32).T
        for h in range(heads):
            vt[h, :, rows] = flipped[h * HEAD : (h + 1) * HEAD, :].astype(BF)

    lse[...] = jnp.zeros_like(lse)

    @pl.loop(0, blocks)
    def _(b):
        rows = pl.ds(pl.multiple_of(b * BLK, BLK), BLK)
        start_row = start[0:1, rows]
        ms[...] = jnp.full_like(ms, -1e30)
        ls[...] = jnp.zeros_like(ls)
        acc[...] = jnp.zeros_like(acc)

        def tile(kb, carry):
            krows = pl.ds(pl.multiple_of(kb * BLK, BLK), BLK)
            mask = tile_mask(start_row, b, kb)
            for h in range(heads):
                first, last = head_window(h)
                qm = jnp.where(head_mask(h, BLK), qs[rows, first:last], 0)
                s = dot_nt(ks[krows, first:last], qm) * scale2
                s = jnp.where(mask, s, -1e30)
                old = ms[h : h + 1, :]
                new = jnp.maximum(old, jnp.max(s, axis=0, keepdims=True))
                p = jnp.exp2(s - new)
                p = jnp.where(mask, p, 0.0)
                fade = jnp.exp2(old - new)
                ms[h : h + 1, :] = new
                ls[h : h + 1, :] = ls[h : h + 1, :] * fade + jnp.sum(p, axis=0, keepdims=True)
                acc[h] = acc[h] * fade + jnp.dot(
                    vt[h, :, krows], p.astype(BF), preferred_element_type=F32
                )
            return carry

        lax.fori_loop(meta[1 + b], b + 1, tile, 0)
        for h in range(heads):
            total = ls[h : h + 1, :]
            lse[h : h + 1, rows] = ms[h : h + 1, :] + jnp.log(total) * math.log2(math.e)
            ot[h * HEAD : (h + 1) * HEAD, :] = acc[h] / total
        os[rows, :] = ot[...].T.astype(BF)

    stage_out(rank, os, out, shard, width)


def attn_bwd_kernel(
    heads, shard, meta, start, qs, ks, vs, o, gm, wo, lse, dq, dk, dv,
    os, dos, kt, delta, dqs, dks, dvs, dqt, qm, dm,
):
    seq, width = o.shape
    scale = HEAD ** (-0.5)
    scale2 = scale * math.log2(math.e)
    rank = meta[0]
    blocks = seq // BLK
    stage_in(rank, o, os, shard, width)
    project(rank, gm, shard, width, [(dos, wo, None)])

    @pl.loop(0, blocks)
    def _(b):
        rows = pl.ds(pl.multiple_of(b * BLK, BLK), BLK)
        flipped = (os[rows, :].astype(F32) * dos[rows, :].astype(F32)).T
        for h in range(heads):
            delta[h : h + 1, rows] = jnp.sum(
                flipped[h * HEAD : (h + 1) * HEAD, :], axis=0, keepdims=True
            )

    @pl.loop(0, blocks)
    def _(b):
        rows = pl.ds(pl.multiple_of(b * BLK, BLK), BLK)
        flipped = ks[rows, :].astype(F32).T
        for h in range(heads):
            kt[h, :, rows] = flipped[h * HEAD : (h + 1) * HEAD, :].astype(BF)

    dks[...] = jnp.zeros_like(dks)
    dvs[...] = jnp.zeros_like(dvs)
    dqt[...] = jnp.zeros_like(dqt)

    @pl.loop(0, blocks)
    def _(b):
        rows = pl.ds(pl.multiple_of(b * BLK, BLK), BLK)
        start_row = start[0:1, rows]
        dqt[...] = jnp.zeros_like(dqt)
        for h in range(heads):
            first, last = head_window(h)
            keep = head_mask(h, BLK)
            qm[h, :, : last - first] = jnp.where(keep, qs[rows, first:last], 0)
            dm[h, :, : last - first] = jnp.where(keep, dos[rows, first:last], 0)

        def tile(kb, carry):
            krows = pl.ds(pl.multiple_of(kb * BLK, BLK), BLK)
            mask = tile_mask(start_row, b, kb)
            for h in range(heads):
                first, last = head_window(h)
                qh = qm[h, :, : last - first]
                dh = dm[h, :, : last - first]
                s = dot_nt(ks[krows, first:last], qh) * scale2
                p = jnp.where(mask, jnp.exp2(s - lse[h : h + 1, rows]), 0.0)
                dp = dot_nt(vs[krows, first:last], dh)
                ds = (p * (dp - delta[h : h + 1, rows])).astype(BF)
                dvs[krows, first:last] += jnp.dot(p.astype(BF), dh, preferred_element_type=F32)
                dks[krows, first:last] += jnp.dot(ds, qh, preferred_element_type=F32)
                dqt[h * HEAD : (h + 1) * HEAD, :] += jnp.dot(
                    kt[h, :, krows], ds, preferred_element_type=F32
                )
            return carry

        lax.fori_loop(meta[1 + b], b + 1, tile, 0)
        dqs[rows, :] = (dqt[...].T * scale).astype(BF)

    stage_out(rank, dqs, dq, shard, width)
    for s in range(seq // shard):
        rel = pl.multiple_of((rank ^ s) * shard, 16)
        here = slice(s * shard, (s + 1) * shard)
        dk[pl.ds(rel, shard), :] = (dks[here, :width] * scale).astype(BF)
        dv[pl.ds(rel, shard), :] = dvs[here, :width].astype(BF)


def vmem():
    return pl.BlockSpec(memory_space=pltpu.VMEM)


def smem():
    return pl.BlockSpec(memory_space=pltpu.SMEM)


def attn_cost(seq, width, products):
    return pl.CostEstimate(
        flops=products * seq * seq * width,
        bytes_accessed=8 * seq * width * 2,
        transcendentals=seq * seq * width // (2 * HEAD),
    )


def attn_fwd(meta, start, normed, wq, bias, shard):
    seq, (_, width, _) = normed.shape[0], wq.shape
    heads = width // HEAD
    wide = -(-width // LANES) * LANES
    staged = jax.ShapeDtypeStruct((seq, wide), BF)
    return pl.pallas_call(
        functools.partial(attn_fwd_kernel, heads, shard),
        out_shape=(
            jax.ShapeDtypeStruct((seq, width), BF),
            jax.ShapeDtypeStruct((8, seq), F32),
            staged,
            staged,
            staged,
        ),
        in_specs=[smem()] + [vmem()] * 4,
        out_specs=(vmem(),) * 5,
        scratch_shapes=[
            pltpu.VMEM((heads, HEAD, seq), BF),
            pltpu.VMEM((seq, wide), BF),
            pltpu.VMEM((wide, BLK), F32),
            pltpu.VMEM((8, BLK), F32),
            pltpu.VMEM((8, BLK), F32),
            pltpu.VMEM((heads, HEAD, BLK), F32),
        ],
        cost_estimate=attn_cost(seq, width, 3),
        name="attn_fwd",
    )(meta, start, normed, wq, bias)


def attn_bwd(meta, start, q, k, v, o, gm, wo, lse, shard):
    seq, width = o.shape
    heads = width // HEAD
    wide = q.shape[1]
    grad = jax.ShapeDtypeStruct((seq, width), BF)
    return pl.pallas_call(
        functools.partial(attn_bwd_kernel, heads, shard),
        out_shape=(grad, grad, grad),
        in_specs=[smem()] + [vmem()] * 8,
        out_specs=(vmem(), vmem(), vmem()),
        scratch_shapes=[
            pltpu.VMEM((seq, wide), BF),
            pltpu.VMEM((seq, wide), BF),
            pltpu.VMEM((heads, HEAD, seq), BF),
            pltpu.VMEM((8, seq), F32),
            pltpu.VMEM((seq, wide), BF),
            pltpu.VMEM((seq, wide), F32),
            pltpu.VMEM((seq, wide), F32),
            pltpu.VMEM((wide, BLK), F32),
            pltpu.VMEM((heads, BLK, 2 * LANES), BF),
            pltpu.VMEM((heads, BLK, 2 * LANES), BF),
        ],
        cost_estimate=attn_cost(seq, width, 8),
        name="attn_bwd",
    )(meta, start, q, k, v, o, gm, wo, lse)


MESH = pl.DeviceIdType.MESH
CHUNKS = 2
STEP = 32


class Place:
    def __init__(self, columns):
        d, t = lax.axis_index("dp"), lax.axis_index("tensor")
        core, low, high = lax.rem(d, 2), lax.rem(t, 2), lax.div(t, 2)
        self.d, self.t, self.columns = d, t, columns
        self.bits = columns.bit_length() - 1
        self.core = (d + 1 - 2 * core, t)
        self.near = (d, t + 1 - 2 * low)
        self.far = (d, t + 2 - 4 * high)
        self.swap = (d + 1 - 2 * core, t + 2 - 4 * high)
        self.home = core == high
        self.away = core != high

    def bit(self, b):
        return lax.rem(lax.div(self.d, 2 << b), 2)

    def column(self, m):
        d = self.d
        for b in range(self.bits):
            if (m >> b) & 1:
                d = d + (2 << b) * (1 - 2 * self.bit(b))
        return (d, self.t)


class Link:
    def __init__(self, send_sems, recv_sems):
        self.send_sems, self.recv_sems = send_sems, recv_sems
        self.count = 0
        self.open, self.kept, self.number = [], [], {}

    def make(self, src, dst, to, like=None):
        if like is None:
            i = self.count
            self.count += 1
        else:
            i = self.number[id(like)]
        copy = pltpu.make_async_remote_copy(
            src_ref=src,
            dst_ref=dst,
            send_sem=self.send_sems.at[i],
            recv_sem=self.recv_sems.at[i],
            device_id=to,
            device_id_type=MESH,
        )
        self.number[id(copy)] = i
        self.kept.append(copy)
        return copy

    def start(self, copy, when=None):
        if when is None:
            copy.start()
        else:
            pl.when(when)(copy.start)
        self.open.append((copy, when))

    def send(self, src, dst, to, when=None):
        copy = self.make(src, dst, to)
        self.start(copy, when)
        return copy

    def close(self):
        for copy, when in self.open:
            if when is None:
                copy.wait_send()
            else:
                pl.when(when)(copy.wait_send)


def arrive(copy, when=None):
    if when is None:
        copy.wait_recv()
    else:
        pl.when(when)(copy.wait_recv)


def meet(partners):
    barrier = pltpu.get_barrier_semaphore()
    for to in partners:
        pl.semaphore_signal(barrier, inc=1, device_id=to, device_id_type=MESH)
    pl.semaphore_wait(barrier, len(partners))


def row_of(ref):
    return ref[...][None, :]


def rows_of(ref, first, count):
    return ref.at[pl.ds(first, count)]


def gather_start(link, place, full, shard, i):
    n = shard // CHUNKS
    near = link.send(rows_of(full, i * n, n), rows_of(full, shard + i * n, n), place.near)
    core = link.send(rows_of(full, i * n, n), rows_of(full, 2 * shard + i * n, n), place.core)
    return near, core


def gather_relay(link, place, full, shard, i, near):
    n = shard // CHUNKS
    near.wait_recv()
    return link.send(
        rows_of(full, shard + i * n, n), rows_of(full, 3 * shard + i * n, n), place.core
    )


class Scatter:
    def __init__(self, link, place, make, part, core_buf, out_buf, near_buf, shard):
        self.link, self.place, self.make, self.part = link, place, make, part
        self.core_buf, self.out_buf, self.near_buf = core_buf, out_buf, near_buf
        self.shard, self.n = shard, shard // CHUNKS
        self.core, self.near = {}, {}

    def fill(self, block):
        rows = pl.ds(pl.multiple_of(block * self.shard, 16), self.shard)
        self.part[rows, :] = self.make(rows).astype(BF)

    def to_core(self, block):
        for i in range(CHUNKS):
            at = (block - 2) * self.shard + i * self.n
            self.core[block - 2, i] = self.link.send(
                rows_of(self.part, 2 * self.shard + at, self.n),
                rows_of(self.core_buf, at, self.n),
                self.place.core,
            )

    def start(self):
        self.fill(3)
        self.to_core(3)
        self.fill(1)

    def rest(self):
        @pl.loop(0, 2)
        def _(b):
            self.fill(2 - 2 * b)

        self.to_core(2)

    def pass_on(self, i):
        at = self.shard + i * self.n
        self.core[1, i].wait_recv()

        @pl.loop(0, self.n // STEP)
        def _(r):
            here = pl.multiple_of(at + r * STEP, STEP)
            there = pl.multiple_of(i * self.n + r * STEP, STEP)
            total = self.part[pl.ds(here, STEP), :].astype(F32) + self.core_buf[
                pl.ds(here, STEP), :
            ].astype(F32)
            self.out_buf[pl.ds(there, STEP), :] = total.astype(BF)

        self.near[i] = self.link.send(
            rows_of(self.out_buf, i * self.n, self.n),
            rows_of(self.near_buf, i * self.n, self.n),
            self.place.near,
        )

    def pair(self, rows):
        return self.part[rows, :].astype(F32) + self.core_buf[rows, :].astype(F32)

    def ready(self, i):
        self.core[0, i].wait_recv()
        self.near[i].wait_recv()

    def rows(self, rows):
        return (
            self.part[rows, :].astype(F32)
            + self.core_buf[rows, :].astype(F32)
            + self.near_buf[rows, :].astype(F32)
        )


class Spread:
    def __init__(self, link, place, src, dst):
        self.link, self.place, self.src, self.dst = link, place, src, dst
        rows = src.shape[-2]
        self.unit = rows // (16 * place.columns) * 16
        self.rest = rows - self.unit * place.columns
        self.at = pl.multiple_of(lax.div(place.d, 2) * self.unit, 16)
        self.pieces, self.shared = [], []

    def cut(self, ref, at, count):
        return ref.at[:, pl.ds(at, count)] if len(ref.shape) == 3 else ref.at[pl.ds(at, count)]

    def move(self, src, at, count, to, when):
        return self.link.send(self.cut(src, at, count), self.cut(self.dst, at, count), to, when)

    def open(self):
        far, home = self.place.far, self.place.home
        if self.unit:
            self.first = self.move(self.src, self.at, self.unit, far, home)
        if self.rest:
            at = self.unit * self.place.columns
            self.pieces.append(self.move(self.src, at, self.rest, far, home))

    def share(self):
        away = self.place.away
        if self.unit:
            arrive(self.first, away)
            for m in range(1, self.place.columns):
                to = self.place.column(m)
                self.pieces.append(self.move(self.dst, self.at, self.unit, to, away))

    def drain(self):
        for copy in self.pieces:
            arrive(copy, self.place.away)


class Local:
    def __init__(self, sems, when=None, base=0):
        self.sems, self.when, self.base, self.copies = sems, when, base, []

    def keep(self, src, dst):
        copy = pltpu.make_async_copy(src, dst, self.sems.at[self.base + len(self.copies)])
        self.copies.append(copy)
        self.run(copy.start)
        return copy

    def run(self, act):
        if self.when is None:
            act()
        else:
            pl.when(self.when)(act)

    def drain(self, first=0):
        for copy in self.copies[first:]:
            self.run(copy.wait)


def pack(local, sources, buf):
    block = buf.shape[0] // len(sources)
    for j, src in enumerate(sources):
        count = src.shape[0]
        local.keep(src, rows_of(buf, j * block, count))
        if count < block:
            buf[j * block + count : (j + 1) * block, :] = jnp.zeros((block - count, buf.shape[1]), buf.dtype)


def scatter_scratch(shard, model):
    return [
        pltpu.VMEM((4 * shard, model), BF),
        pltpu.VMEM((2 * shard, model), BF),
        pltpu.VMEM((shard, model), BF),
        pltpu.VMEM((shard, model), BF),
    ]


def over_rows(first, count, step, fn):
    @pl.loop(0, count // step)
    def _(r):
        fn(pl.ds(pl.multiple_of(first + r * step, 16), step))


class Halving:
    def __init__(self, link, place, source, first, size, turn, work, got):
        self.link, self.place = link, place
        self.source, self.first, self.size = source, first, size
        self.order = [(b + turn) % place.bits for b in range(place.bits)]
        self.work, self.got = work, got
        self.copies = []

    def start(self, s):
        n = self.size >> (s + 1)
        bit = self.place.bit(self.order[s])
        src, base = (self.source, self.first) if s == 0 else (self.work[s - 1], 0)
        at = pl.multiple_of(base + (1 - bit) * n, 16)
        self.copies.append(
            self.link.send(
                rows_of(src, at, n), self.got[s], self.place.column(1 << self.order[s])
            )
        )

    def finish(self, s):
        n = self.size >> (s + 1)
        bit = self.place.bit(self.order[s])
        src, base = (self.source, self.first) if s == 0 else (self.work[s - 1], 0)
        self.copies[s].wait_recv()

        @pl.loop(0, n // 16)
        def _(r):
            here = pl.multiple_of(base + bit * n + r * 16, 16)
            to = pl.ds(pl.multiple_of(r * 16, 16), 16)
            total = src[pl.ds(here, 16), :].astype(F32) + self.got[s][to, :].astype(F32)
            self.work[s][to, :] = total.astype(BF)

    def offset(self):
        at, n = 0, self.size
        for b in self.order:
            n //= 2
            at = at + self.place.bit(b) * n
        return self.first + at


def halving_scratch(size, bits, model):
    return [pltpu.VMEM((size >> (s + 1), model), BF) for s in range(bits)]


class Doubling:
    def __init__(self, link, place, half, full, slice_ref, far_buf):
        self.link, self.place, self.half, self.full = link, place, half, full
        self.far = None
        self.slice_ref, self.far_buf = slice_ref, far_buf
        self.n = half.size >> place.bits
        self.at = half.offset()
        self.cores, self.waits = [], []

    def start(self):
        self.far = self.link.send(
            self.slice_ref, self.far_buf, self.place.far, self.place.away
        )

    def to_core(self, at, n):
        self.link.send(
            rows_of(self.full, at, n), rows_of(self.full, at, n), self.place.core, self.place.home
        )

    def join(self):
        if self.far is not None:
            arrive(self.far, self.place.home)

        @pl.when(self.place.home)
        def _():
            @pl.loop(0, self.n // 16)
            def _(r):
                here = pl.ds(pl.multiple_of(r * 16, 16), 16)
                to = pl.ds(pl.multiple_of(self.at + r * 16, 16), 16)
                total = self.slice_ref[here, :].astype(F32) + self.far_buf[here, :].astype(F32)
                self.full[to, :] = total.astype(BF)

        self.block, self.count = pl.multiple_of(self.at, 16), self.n
        self.stage = 0
        self.push(self.block)

    def push(self, fresh):
        if self.stage < self.place.bits:
            b = self.half.order[self.place.bits - 1 - self.stage]
            self.copy = self.link.send(
                rows_of(self.full, self.block, self.count),
                rows_of(self.full, self.block, self.count),
                self.place.column(1 << b),
                self.place.home,
            )
        copy = self.link.send(
            rows_of(self.full, fresh, self.count if self.stage == 0 else self.count // 2),
            rows_of(self.full, fresh, self.count if self.stage == 0 else self.count // 2),
            self.place.core,
            self.place.home,
        )
        self.cores.append(copy)

    def advance(self):
        b = self.half.order[self.place.bits - 1 - self.stage]
        bit = self.place.bit(b)
        fresh = pl.multiple_of(self.block + (1 - 2 * bit) * self.count, 16)
        arrive(self.copy, self.place.home)
        self.block = pl.multiple_of(self.block - bit * self.count, 16)
        self.count *= 2
        self.stage += 1
        self.push(fresh)


def norm_stats(values):
    center = values - jnp.mean(values, axis=-1, keepdims=True)
    rstd = lax.rsqrt(jnp.mean(center * center, axis=-1, keepdims=True) + EPS)
    return center * rstd, rstd


def norm_pull(grad, hat, rstd, gain):
    gn = grad * gain
    return rstd * (
        gn
        - jnp.mean(gn, axis=-1, keepdims=True)
        - hat * jnp.mean(gn * hat, axis=-1, keepdims=True)
    )


def enter_kernel(
    columns, shard, hid, cot, ids, qv, ub, wq, wo, gain, shift,
    own, full, cot_own, ids_o, qv_o, ub_o, wq_o, wo_o, send_sems, recv_sems, local_sems,
):
    place, link = Place(columns), Link(send_sems, recv_sems)
    n = shard // CHUNKS
    home, away = place.home, place.away
    meet([place.core, place.near, place.far, place.swap] + [place.column(m) for m in range(1, columns)])
    weights = [Spread(link, place, wq, wq_o), Spread(link, place, wo, wo_o)]

    ids_copy = link.send(ids, ids_o, place.swap, away)
    swaps = [
        link.send(rows_of(hid, i * n, n), rows_of(own, i * n, n), place.swap, away) for i in range(CHUNKS)
    ]
    for weight in weights:
        weight.open()
    qv_copy = link.send(qv, qv_o, place.far, home)
    ub_copy = link.send(ub, ub_o, place.far, home)
    local = Local(local_sems, home)
    held = [local.keep(rows_of(hid, i * n, n), rows_of(own, i * n, n)) for i in range(CHUNKS)]
    local.keep(cot, cot_own)
    local.keep(wq, wq_o)
    local.keep(wo, wo_o)
    local.keep(ids, ids_o)
    local.keep(qv, qv_o)
    local.keep(ub, ub_o)

    near, core = {}, []
    for i in range(CHUNKS):
        pl.when(home)(held[i].wait)
        arrive(swaps[i], away)

        def rows(here):
            hat = norm_stats(own[here, :].astype(F32))[0]
            full[here, :] = (hat * row_of(gain) + row_of(shift)).astype(BF)

        over_rows(i * n, n, STEP, rows)
        near[i], copy = gather_start(link, place, full, shard, i)
        core.append(copy)
    cot_copy = link.send(cot, cot_own, place.swap, away)
    for i in range(CHUNKS):
        core.append(gather_relay(link, place, full, shard, i, near[i]))
    for weight in weights:
        weight.share()
    for copy in core:
        copy.wait_recv()
    for weight in weights:
        weight.drain()
    for copy in (ids_copy, qv_copy, ub_copy, cot_copy):
        arrive(copy, away)
    local.drain(CHUNKS)
    link.close()


def mid_kernel(
    columns, shard, att, wo, own, bias, gain, shift, wu, wd, pieces, cot_own, cot_near,
    mid, full, cfull, wu_o, wd_o,
    part, core_buf, out_buf, near_buf, send_sems, recv_sems, local_sems
):
    place, link = Place(columns), Link(send_sems, recv_sems)
    n = shard // CHUNKS
    home, away = place.home, place.away
    unit, rest = pieces_of(wu, columns)
    at = pl.multiple_of(lax.div(place.d, 2) * unit, 16)
    mine = Local(local_sems, home, 0)
    mine.keep(wu, wu_o)
    mine.keep(wd, wd_o)
    both = Local(local_sems, None, 2)
    both.keep(cot_own, rows_of(cfull, 0, shard))
    both.keep(cot_near, rows_of(cfull, shard, shard))
    other = Local(local_sems, away, 4)
    for j, out in enumerate((wu_o, wd_o)):
        if unit:
            other.keep(rows_of(pieces, j * unit, unit), rows_of(out, at, unit))
        if rest:
            last = rows_of(pieces, 2 * unit + j * rest, rest)
            other.keep(last, rows_of(out, unit * columns, rest))
    meet([place.core, place.near, place.far] + [place.column(m) for m in range(1, columns)])
    shared = []
    if unit:
        for j, out in enumerate((wu_o, wd_o)):
            for m in range(1, columns):
                src = rows_of(pieces, j * unit, unit)
                shared.append(link.send(src, rows_of(out, at, unit), place.column(m), away))

    def make(rows):
        return mm(att[rows, :], wo[...])

    total = Scatter(link, place, make, part, core_buf, out_buf, near_buf, shard)
    total.start()
    for i in range(CHUNKS):
        total.pass_on(i)
    total.rest()
    core = [
        link.send(cot_own, rows_of(cfull, 2 * shard, shard), place.core),
        link.send(cot_near, rows_of(cfull, 3 * shard, shard), place.core),
    ]
    near = {}
    for i in range(CHUNKS):
        total.ready(i)

        def rows(here):
            value = own[here, :].astype(F32) + total.rows(here) + row_of(bias)
            mid[here, :] = value
            full[here, :] = (norm_stats(value)[0] * row_of(gain) + row_of(shift)).astype(BF)

        over_rows(i * n, n, STEP, rows)
        near[i], copy = gather_start(link, place, full, shard, i)
        core.append(copy)
    for i in range(CHUNKS):
        core.append(gather_relay(link, place, full, shard, i, near[i]))
    for copy in core:
        copy.wait_recv()
    for copy in shared:
        arrive(copy, away)
    for local in (mine, both, other):
        local.drain()
    link.close()


def pieces_of(weight, columns):
    rows = weight.shape[0]
    unit = rows // (16 * columns) * 16
    return unit, rows - unit * columns


def back_kernel(
    columns, shard, gi, wu, act, wd, raw_u, raw_d, mid, cot_full, gain, bias, *refs
):
    place, link = Place(columns), Link(*refs[-3:-1])
    bits = place.bits
    gmid, full, res, res_near, slices, sums = refs[:6]
    scratch = list(refs[6:-3])
    a_bufs, b_bufs = scratch[:4], scratch[4:6]
    cot, grads_u, grads_d = scratch[6:9]
    halves = scratch[9:]
    n = shard // CHUNKS
    local = Local(refs[-1])
    pack(local, [raw_u], grads_u)
    pack(local, [raw_d], grads_d)
    local.keep(rows_of(cot_full, 0, shard), cot)
    meet([place.core, place.near] + [place.column(1 << b) for b in range(bits)])

    def make(rows):
        return mm_nt(gi[rows, :], wu[...])

    def make2(rows):
        return mm(act[rows, :], wd[...])

    total = Scatter(link, place, make, *a_bufs, shard)
    total2 = Scatter(link, place, make2, *b_bufs, None, None, shard)
    size = grads_u.shape[0]
    slice_u, slice_d = (rows_of(slices, j * (size // columns), size // columns) for j in range(2))
    half_u = Halving(
        link, place, grads_u, 0, size, 0, halves[: bits - 1] + [slice_u], halves[bits - 1 : 2 * bits - 1]
    )
    halves = halves[2 * bits - 1 :]
    half_d = Halving(
        link, place, grads_d, 0, size, 1, halves[: bits - 1] + [slice_d], halves[bits - 1 : 2 * bits - 1]
    )
    local.drain()
    half_u.start(0)
    half_d.start(0)
    total.start()
    for i in range(CHUNKS):
        total.pass_on(i)
    total.rest()
    total2.start()
    total2.rest()
    for copy in total2.core.values():
        copy.wait_recv()

    def rows2(here):
        res[here, :] = mid[here, :] + total2.pair(here) + row_of(bias)

    def rows3(here):
        there = pl.ds(pl.multiple_of(here.start - shard, STEP), STEP)
        res_near[there, :] = total2.pair(here).astype(BF)

    over_rows(0, shard, STEP, rows2)
    over_rows(shard, shard, STEP, rows3)
    sums[...] = jnp.zeros_like(sums)
    near, core = {}, []
    for i in range(CHUNKS):
        total.ready(i)

        def rows(here):
            grad = total.rows(here)
            out_grad = cot[here, :].astype(F32)
            hat, rstd = norm_stats(mid[here, :])
            value = out_grad + norm_pull(grad, hat, rstd, row_of(gain))
            gmid[here, :] = value
            full[here, :] = value.astype(BF)
            for row, term in enumerate((value, grad * hat, grad, out_grad)):
                sums[row : row + 1, :] += jnp.sum(term, axis=0, keepdims=True)

        over_rows(i * n, n, STEP, rows)
        near[i], copy = gather_start(link, place, full, shard, i)
        core.append(copy)
    half_u.finish(0)
    half_d.finish(0)
    if bits > 1:
        half_u.start(1)
        half_d.start(1)
    for i in range(CHUNKS):
        core.append(gather_relay(link, place, full, shard, i, near[i]))
    for s in range(1, bits):
        half_u.finish(s)
        if s + 1 < bits:
            half_u.start(s + 1)
        half_d.finish(s)
        if s + 1 < bits:
            half_d.start(s + 1)
    for copy in core:
        copy.wait_recv()
    link.close()


def exit_kernel(
    columns, shard, dq, dk, dv, wq, own, gmid, slices, far, res, res_near, gq, gk, gv, go, small_in, gain, *refs
):
    place, link = Place(columns), Link(*refs[-3:-1])
    bits = place.bits
    inp, out, full_u, full_d, full_a, small = refs[:6]
    scratch = list(refs[6:-3])
    a_bufs = scratch[:4]
    swap_buf, out_buf, far_a0, far_a1, grads_a = scratch[4:9]
    steps = bits + 3
    sum_own, sum_got = scratch[9 : 9 + steps], scratch[9 + steps : 9 + 2 * steps]
    halves = scratch[9 + 2 * steps :]
    n = shard // CHUNKS
    local = Local(refs[-1])
    pack(local, [gq, gk, gv, go], grads_a)
    hops = [place.core] + [place.column(1 << b) for b in range(bits)] + [place.near, place.far]
    meet(hops + [place.swap])
    size = full_u.shape[0]

    def make(rows):
        return mm(dq[rows, :], wq[0]) + mm(dk[rows, :], wq[1]) + mm(dv[rows, :], wq[2])

    total = Scatter(link, place, make, *a_bufs, shard)
    half_a = []
    for side in range(2):
        half_a.append(
            Halving(
                link, place, grads_a, side * (size // 2), size // 2, side,
                halves[:bits], halves[bits : 2 * bits],
            )
        )
        halves = halves[2 * bits :]
    half_u = Halving(link, place, None, 0, size, 0, [], [])
    half_d = Halving(link, place, None, 0, size, 1, [], [])
    held = size // columns
    double = [
        Doubling(link, place, half_u, full_u, rows_of(slices, 0, held), rows_of(far, 0, held)),
        Doubling(link, place, half_d, full_d, rows_of(slices, held, held), rows_of(far, held, held)),
        Doubling(link, place, half_a[0], full_a, half_a[0].work[bits - 1], far_a0),
        Doubling(link, place, half_a[1], full_a, half_a[1].work[bits - 1], far_a1),
    ]
    local.drain()
    half_a[0].start(0)
    half_a[1].start(0)
    total.start()
    for i in range(CHUNKS):
        total.pass_on(i)
    total.rest()

    def finish_out(here):
        value = (res[here, :] + res_near[here, :].astype(F32)).astype(BF)
        out_buf[here, :] = value

        @pl.when(place.home)
        def _():
            out[here, :] = value

    over_rows(0, shard, STEP, finish_out)
    swaps = [link.send(out_buf, out, place.swap, place.away)]
    sum_own[0][...] = small_in[...]
    for s in range(bits):
        for half in half_a:
            half.finish(s)
            if s + 1 < bits:
                half.start(s + 1)
    double[2].start()
    double[3].start()
    double[0].join()
    double[1].join()
    for i in range(CHUNKS):
        total.ready(i)

        def rows(here):
            grad = total.rows(here)
            hat, rstd = norm_stats(own[here, :].astype(F32))
            value = (gmid[here, :] + norm_pull(grad, hat, rstd, row_of(gain))).astype(BF)
            swap_buf[here, :] = value
            for row, term in enumerate((grad * hat, grad)):
                sum_own[0][row : row + 1, :] += jnp.sum(term, axis=0, keepdims=True)

            @pl.when(place.home)
            def _():
                inp[here, :] = value

        over_rows(i * n, n, STEP, rows)
        swaps.append(
            link.send(rows_of(swap_buf, i * n, n), rows_of(inp, i * n, n), place.swap, place.away)
        )
    hop_copies = [link.send(sum_own[0], sum_got[0], hops[0])]

    def next_hop(s):
        hop_copies[s].wait_recv()
        into = small if s + 1 == steps else sum_own[s + 1]
        into[...] = sum_own[s][...] + sum_got[s][...]
        if s + 1 < steps:
            hop_copies.append(link.send(sum_own[s + 1], sum_got[s + 1], hops[s + 1]))

    hop = 0
    for s in range(bits):
        double[0].advance()
        double[1].advance()
        if s == 0:
            double[2].join()
            double[3].join()
        else:
            double[2].advance()
            double[3].advance()
        if hop < steps:
            next_hop(hop)
            hop += 1
    double[2].advance()
    double[3].advance()
    while hop < steps:
        next_hop(hop)
        hop += 1
    for one in double:
        for copy in one.cores:
            arrive(copy, place.away)
    for copy in swaps:
        arrive(copy, place.away)
    link.close()


def any_space():
    return pl.BlockSpec(memory_space=pl.ANY)


SEMS = 160


def sems(local=8):
    return [
        pltpu.SemaphoreType.DMA((SEMS,)),
        pltpu.SemaphoreType.DMA((SEMS,)),
        pltpu.SemaphoreType.DMA((local,)),
    ]


def remote_call(name, kernel, number, outs, in_specs, scratch):
    return pl.pallas_call(
        kernel,
        out_shape=outs,
        in_specs=in_specs,
        out_specs=jax.tree.map(lambda _: vmem(), outs),
        scratch_shapes=scratch + sems(),
        compiler_params=pltpu.CompilerParams(
            collective_id=number, has_side_effects=True, vmem_limit_bytes=62 << 20
        ),
        name=name,
    )


def shaped(shape, dtype):
    return jax.ShapeDtypeStruct(shape, dtype)


def like(x):
    return shaped(x.shape, x.dtype)


def enter(columns, hid, cot, ids, qv, ub, wq, wo, *vecs):
    shard, model = hid.shape
    outs = (like(hid), shaped((4 * shard, model), BF), like(cot), like(ids), like(qv), like(ub), like(wq), like(wo))
    call = remote_call(
        "enter", functools.partial(enter_kernel, columns, shard), 0, outs, [any_space()] * 7 + [vmem()] * 2, []
    )
    return call(hid, cot, ids, qv, ub, wq, wo, *vecs)


def make_mid(columns, att, wo, own, vecs, wu, wd, pieces, cot_own, cot_near):
    shard, model = own.shape
    whole = shaped((4 * shard, model), BF)
    outs = (shaped((shard, model), F32), whole, whole, like(wu), like(wd))
    call = remote_call(
        "mid", functools.partial(mid_kernel, columns, shard), 1, outs, [vmem()] * 6 + [any_space()] * 5,
        scatter_scratch(shard, model),
    )
    return call(att, wo, own, *vecs, wu, wd, pieces, cot_own, cot_near)


def make_back(columns, size, gi, wu, act, wd, grads_u, grads_d, mid, cot, *vecs):
    shard, model = mid.shape
    bits = columns.bit_length() - 1
    outs = (
        shaped((shard, model), F32),
        shaped((4 * shard, model), BF),
        shaped((shard, model), F32),
        shaped((shard, model), BF),
        shaped((2 * (size // columns), model), BF),
        shaped((8, model), F32),
    )
    per_side = halving_scratch(size, bits, model)
    halves = per_side[: bits - 1] + per_side
    call = remote_call(
        "back", functools.partial(back_kernel, columns, shard), 2, outs,
        [vmem()] * 4 + [any_space()] * 2 + [vmem(), any_space(), vmem(), vmem()],
        scatter_scratch(shard, model)
        + scatter_scratch(shard, model)[:2]
        + [pltpu.VMEM((shard, model), BF)]
        + [pltpu.VMEM((size, model), BF)] * 2
        + halves
        + halves,
    )
    return call(gi, wu, act, wd, grads_u, grads_d, mid, cot, *vecs)


def make_exit(columns, size, dq, dk, dv, wq, own, gmid, slices, far, res, res_near, grads, small, vec):
    shard, model = own.shape
    bits = columns.bit_length() - 1
    outs = (
        shaped((shard, model), BF),
        shaped((shard, model), BF),
        shaped((size, model), BF),
        shaped((size, model), BF),
        shaped((size, model), BF),
        shaped(small.shape, F32),
    )
    n = size // columns
    per_side = halving_scratch(size // 2, bits, model)
    steps = bits + 3
    call = remote_call(
        "exit", functools.partial(exit_kernel, columns, shard), 3, outs,
        [vmem()] * 10 + [any_space()] * 4 + [vmem()] * 2,
        scatter_scratch(shard, model)
        + [
            pltpu.VMEM((shard, model), BF),
            pltpu.VMEM((shard, model), BF),
            pltpu.VMEM((n // 2, model), BF),
            pltpu.VMEM((n // 2, model), BF),
            pltpu.VMEM((size, model), BF),
        ]
        + [pltpu.VMEM(small.shape, F32)] * (2 * steps)
        + (per_side + per_side) * 2,
    )
    return call(dq, dk, dv, wq, own, gmid, slices, far, res, res_near, *grads, small, vec)


def body(
    hidden,
    segment_ids,
    lengths,
    norm1_gain,
    norm1_shift,
    qkv_weight,
    qv_bias,
    out_weight,
    out_bias,
    norm2_gain,
    norm2_shift,
    up_weight,
    up_bias,
    down_weight,
    down_bias,
    cotangent,
):
    _, shard, model = hidden.shape
    seq = segment_ids.shape[1]
    width = qkv_weight.shape[2]
    d, t = lax.axis_index("dp"), lax.axis_index("tensor")
    columns = lax.axis_size("dp") // 2
    rank = 2 * (d & 1) + (t & 1)

    places = jnp.arange(seq, dtype=jnp.int32)
    ids = jnp.where(places < lengths[0], segment_ids[0], 16 + places)
    start = jnp.sum((ids[None, :] < ids[:, None]).astype(jnp.int32), axis=1)
    blocks = seq // BLK
    start = jnp.concatenate([start, start[::BLK] // BLK, jnp.zeros((LANES - blocks,), jnp.int32)])
    start = start[None]

    own, normed1, cot_own, start, b_qv, b_up, w_qkv, w_out = enter(
        columns, hidden[0], cotangent[0], start, qv_bias, up_bias, jnp.swapaxes(qkv_weight, 1, 2), out_weight,
        norm1_gain, norm1_shift,
    )
    everywhere = [(i, j) for i in range(2 * columns) for j in range(4)]
    to_near = [(4 * i + j, 4 * i + (j ^ 1)) for i, j in everywhere]
    to_away = [(4 * i + j, 4 * i + (j ^ 2)) for i, j in everywhere if i % 2 == j // 2]
    to_home = [(4 * i + j, 4 * i + (j ^ 2)) for i, j in everywhere if i % 2 != j // 2]
    axes = ("dp", "tensor")
    unit, rest = pieces_of(up_weight, columns)
    pieces = [lax.dynamic_slice_in_dim(w, (d // 2) * unit, unit, 0) for w in (up_weight, down_weight)]
    pieces += [w[unit * columns :] for w in (up_weight, down_weight)]
    cot_own, pieces, normed1 = lax.optimization_barrier((cot_own, jnp.concatenate(pieces), normed1))
    cot_near = lax.ppermute(cot_own, axes, to_near)
    pieces = lax.ppermute(pieces, axes, to_away)

    meta = jnp.concatenate([rank[None].astype(jnp.int32), start[0, seq : seq + blocks]])

    attended, lse, q, k, v = attn_fwd(meta, start, normed1, w_qkv, b_qv, shard)

    mid, normed2, cot_full, w_up, w_down = make_mid(
        columns,
        attended,
        w_out,
        own,
        (out_bias, norm2_gain, norm2_shift),
        up_weight,
        down_weight,
        pieces,
        cot_own,
        cot_near,
    )
    inner = mm(normed2, w_up) + b_up
    c0 = math.sqrt(2.0 / math.pi)
    tanh = jnp.tanh(c0 * (inner + 0.044715 * inner * inner * inner))
    active = (0.5 * inner * (1.0 + tanh)).astype(BF)
    slope = 0.5 * (1.0 + tanh) + 0.5 * inner * (1.0 - tanh * tanh) * c0 * (
        1.0 + 3 * 0.044715 * inner * inner
    )
    grad_inner = (mm_nt(cot_full, w_down) * slope).astype(BF)
    unit = 32 * columns
    size = -(-model // unit) * unit
    grad_mid, gm_full, res, res_near, slices, sums = make_back(
        columns,
        size,
        grad_inner,
        w_up,
        active,
        w_down,
        mm_tn(normed2, grad_inner).astype(BF),
        mm_tn(active, cot_full).astype(BF),
        mid,
        cot_full,
        norm2_gain,
        down_bias,
    )
    far = lax.ppermute(slices, axes, to_home)
    res_near = lax.ppermute(res_near, axes, to_near)
    dq, dk, dv = attn_bwd(meta, start, q, k, v, attended, gm_full, w_out, lse, shard)
    far, dk, dv = lax.optimization_barrier((far, dk, dv))
    res_near, dq = lax.optimization_barrier((res_near, dq))
    att_grads = [
        mm_tn(dq, normed1).astype(BF),
        mm_tn(dk, normed1).astype(BF),
        mm_tn(dv, normed1).astype(BF),
        mm_tn(attended, gm_full).astype(BF),
    ]

    qv_grad = jnp.concatenate([jnp.sum(dq, axis=0, dtype=F32), jnp.sum(dv, axis=0, dtype=F32)])
    qv_grad = jnp.pad(qv_grad, (0, model - 2 * width))
    up_b_grad = jnp.sum(grad_inner, axis=0, dtype=F32)
    slots = lax.broadcasted_iota(jnp.int32, (4, 1), 0) == rank
    small = jnp.concatenate(
        [
            jnp.zeros((2, model), F32),
            sums[:4],
            jnp.zeros((2, model), F32),
            jnp.where(slots, up_b_grad[None], 0.0),
            jnp.where(slots, qv_grad[None], 0.0),
        ]
    )
    input_grad, output, up_grad, down_grad, att_grad, small = make_exit(
        columns,
        size,
        dq,
        dk,
        dv,
        w_qkv,
        own,
        grad_mid,
        slices,
        far,
        res,
        res_near,
        att_grads,
        small,
        norm1_gain,
    )
    quarter = lax.dynamic_slice_in_dim(small, 12 + t, 1, 0)[0, : 2 * width].reshape(2, width)
    att_grad = att_grad.reshape(4, size // 4, model)
    qkv_grad = att_grad[:3, :width].astype(F32)
    return (
        output[None],
        input_grad[None],
        small[0],
        small[1],
        jnp.swapaxes(qkv_grad, 1, 2),
        quarter,
        att_grad[3, :width].astype(F32),
        small[2],
        small[3],
        small[4],
        up_grad[:model].astype(F32),
        lax.dynamic_slice_in_dim(small, 8 + t, 1, 0)[0],
        down_grad[:model].astype(F32),
        small[5],
    )


def solution(mesh):
    in_specs = (
        P("dp", "tensor", None),
        P("dp", None),
        P("dp"),
        P(),
        P(),
        P(None, None, "tensor"),
        P(None, "tensor"),
        P("tensor", None),
        P(),
        P(),
        P(),
        P(None, "tensor"),
        P("tensor"),
        P("tensor", None),
        P(),
        P("dp", "tensor", None),
    )
    out_specs = (
        P("dp", "tensor", None),
        P("dp", "tensor", None),
        P(),
        P(),
        P(None, None, "tensor"),
        P(None, "tensor"),
        P("tensor", None),
        P(),
        P(),
        P(),
        P(None, "tensor"),
        P("tensor"),
        P("tensor", None),
        P(),
    )
    return jax.shard_map(body, mesh=mesh, in_specs=in_specs, out_specs=out_specs, check_vma=False)
```

profile of v0, /device:TPU:1, one launch (start us, length us, event | category | flops | bytes accessed | tf_op | source)
XLA Modules:
  0.0 397.6 jit_solution(1959116133886093578)
XLA Ops:
  0.6 0.0 slice-start
  0.7 0.0 slice-start.1
  0.7 1.4 constant_dynamic-slice_fusion
  2.7 0.7 fusion.8
  3.5 0.8 convert_reduce_fusion
  4.3 0.1 slice.48
  4.4 0.1 concatenate.15
  4.5 0.6 broadcast_in_dim.51.ids
  5.1 0.0 slice-done
  5.1 0.0 slice-done.1
  5.1 0.1 pad_maximum_fusion
  5.2 73.3 %enter.1 = (bf16[320,1120]{1,0:T(8,128)(2,1)}, bf16[1280,1120]{1,0:T(8,128)(2,1)}, bf16[320,1120]{1,0:T(8,128)(2,1)}, s32[1,1408]{1,0:T(1,128)}, f32[2,280]{1,0:...) custom-call(bf16[320,1120]{1,0:T(8,128)(2,1)} %bitcast.38, ...), custom_call_target="tpu_custom_call" | custom-call | tf_op jit(solution)/shard_map/enter/pallas_call | solution.py:1051
  78.5 1.3 collective-permute-start
  79.8 0.1 collective-permute-start.1
  79.9 0.7 slice_bitcast_fusion.1
  80.6 0.6 pad_add_fusion.meta
  81.1 22.1 %attn_fwd.1 = (bf16[1280,280]{1,0:T(8,128)(2,1)}, f32[8,1280]{1,0:T(8,128)}, bf16[1280,384]{1,0:T(8,128)(2,1)}, bf16[1280,384]{1,0:T(8,128)(2,1)}, bf16[1280,384]{1,0:T(8,128)(2,1)}) custom-call(s32[6]{0:T(128)} %pad_add_fusion.meta, s32[1,1408]{1,0:T(1,128)} %get-tuple-element.55.start, bf16[1280,1120]{1,0:T(8,128)(2,1)} %get-tuple-element.58.normed, ...), custom_call_target="tpu_custom_call" | custom-call | flops 1376256000 | bytes 5734400 | tf_op jit(solution)/shard_map/attn_fwd/pallas_call | solution.py:236
  103.3 8.4 %collective-permute-done.1.cot_near = bf16[320,1120]{1,0:T(8,128)(2,1)} collective-permute-done((bf16[320,1120]{1,0:T(8,128)(2,1)}, bf16[320,1120]{1,0:T(8,128)(2,1)}, u32[]{:S(2)}, u32[]{:S(2)}) %collective-permute-start.1) | collective-permute-done | bytes 716832 | tf_op jit(solution)/shard_map/ppermute | solution.py:1167
  111.7 0.0 collective-permute-done.pieces
  111.7 1.1 copy-done.8
  112.8 50.6 %mid.1 = (f32[320,1120]{1,0:T(8,128)}, bf16[1280,1120]{1,0:T(8,128)(2,1)}, bf16[1280,1120]{1,0:T(8,128)(2,1)}, bf16[1120,1120]{1,0:T(8,128)(2,1)}, bf16[1120,1120]{1,0:T(8,128)(2,1)}) custom-call(bf16[1280,280]{1,0:T(8,128)(2,1)} %get-tuple-element.61.att.o, bf16[280,1120]{1,0:T(8,128)(2,1)} %get-tuple-element.62.wo, ...), custom_call_target="tpu_custom_call" | custom-call | tf_op jit(solution)/shard_map/mid/pallas_call | solution.py:1062
  163.4 0.0 copy-done.16
  163.4 0.0 copy-start.2
  163.4 7.7 %multiply_convert_fusion = (bf16[1280,1120]{1,0:T(8,128)(2,1)S(1)}, f32[1280,1120]{1,0:T(8,128)S(1)}) fusion(f32[1120]{0:T(1024)S(1)} %copy-done.16, bf16[1280,1120]{1,0:T(8,128)(2,1)} %get-tuple-element.68, bf16[1120,1120]{1,0:T(8,128)(2,1)} %get-tuple-element.69.wu), kind=kOutput, calls=%fused_computation.14 | convolution fusion | flops 3225600000 | bytes 13982080 | tf_op jit(solution)/shard_map/dot_general | solution.py:20
  171.1 0.0 copy-start.3
  171.1 0.0 copy-done.2
  171.1 0.0 copy-start.5
  171.1 5.5 %convolution_convert_fusion.raw_d = bf16[1120,1120]{1,0:T(8,128)(2,1)} fusion(bf16[1280,1120]{1,0:T(8,128)(2,1)S(1)} %get-tuple-element.107.act, bf16[1280,1120]{1,0:T(8,128)(2,1)S(1)} %copy-done.2), kind=kOutput, calls=%fused_computation.4 | convolution fusion | flops 3212518400 | bytes 8243200 | tf_op jit(solution)/shard_map/dot_general | solution.py:28
  176.6 0.0 copy-done.3
  176.6 0.0 copy-done.5
  176.6 8.9 %convert_reduce_fusion.1 = (f32[1120]{0:T(1024)S(1)}, bf16[1280,1120]{1,0:T(8,128)(2,1)S(1)}) fusion(f32[1280,1120]{1,0:T(8,128)S(1)} %get-tuple-element.108, bf16[1280,1120]{1,0:T(8,128)(2,1)S(1)} %copy-done.2, bf16[1120,1120]{1,0:T(8,128)(2,1)S(1)} %copy-done.5), kind=kOutput, calls=%fused_computation.13 | convolution fusion | flops 3241368576 | bytes 13982080 | tf_op jit(solution)/shard_map/dot_general | solution.py:24
  185.6 0.0 copy-start.4
  185.6 0.0 copy-done.15
  185.6 5.5 %convolution_convert_fusion.1.raw_u = bf16[1120,1120]{1,0:T(8,128)(2,1)} fusion(bf16[1280,1120]{1,0:T(8,128)(2,1)S(1)} %copy-done.15, bf16[1280,1120]{1,0:T(8,128)(2,1)S(1)} %get-tuple-element.110.gi), kind=kOutput, calls=%fused_computation.5 | convolution fusion | flops 3212518400 | bytes 8243200 | tf_op jit(solution)/shard_map/dot_general | solution.py:28
  191.1 0.0 copy-done.4
  191.1 60.1 %back.1 = (f32[320,1120]{1,0:T(8,128)}, bf16[1280,1120]{1,0:T(8,128)(2,1)}, f32[320,1120]{1,0:T(8,128)}, bf16[320,1120]{1,0:T(8,128)(2,1)}, bf16[576,1120]{1,0:T(8,128)(2,1)}, /*index=5*/f32[8,1120]{1,0:T(8,128)}) custom-call(bf16[1280,1120]{1,0:T(8,128)(2,1)} %copy-done.4, bf16[1120,1120]{1,0:T(8,128)(2,1)} %get-tuple-element.69.wu, ...), custom_call_target="tpu_custom_call" | custom-call | tf_op jit(solution)/shard_map/back/pallas_call | solution.py:1088
  251.2 3.3 collective-permute-start.3
  254.5 0.1 collective-permute-start.2
  254.6 0.8 slice.52
  255.3 24.7 %attn_bwd.1 = (bf16[1280,280]{1,0:T(8,128)(2,1)}, bf16[1280,280]{1,0:T(8,128)(2,1)}, bf16[1280,280]{1,0:T(8,128)(2,1)}) custom-call(s32[6]{0:T(128)} %pad_add_fusion.meta, s32[1,1408]{1,0:T(1,128)} %get-tuple-element.55.start, bf16[1280,384]{1,0:T(8,128)(2,1)} %get-tuple-element.73.qs, bf16[1280,384]{1,0:T(8,128)(2,1)} %get-tuple-element.74.ks, ...), custom_call_target="tpu_custom_call" | custom-call | flops 3670016000 | bytes 5734400 | tf_op jit(solution)/shard_map/attn_bwd/pallas_call | solution.py:265
  280.0 0.0 copy-done.11
  280.0 4.0 %convolution_convert_fusion.2.go = bf16[280,1120]{1,0:T(8,128)(2,1)} fusion(bf16[1280,280]{1,0:T(8,128)(2,1)S(1)} %copy-done.11, bf16[1280,1120]{1,0:T(8,128)(2,1)} %get-tuple-element.76.gm), kind=kOutput, calls=%fused_computation.16 | convolution fusion | flops 803129600 | bytes 4211200 | tf_op jit(solution)/shard_map/dot_general | solution.py:28
  284.0 3.0 collective-permute-done.2.res_near
  287.1 0.2 convert_reduce_fusion.3
  287.3 2.0 convolution_convert_fusion.5.gq
  289.3 0.0 collective-permute-done.3.far
  289.3 0.2 convert_reduce_fusion.2
  289.5 2.0 convolution_convert_fusion.3.gv
  291.5 2.0 convolution_convert_fusion.4.gk
  293.5 0.1 select_maximum_fusion
  293.5 0.1 broadcast_select_fusion
  293.6 1.3 concatenate.19.small_in
  294.9 85.8 %exit.1 = (bf16[320,1120]{1,0:T(8,128)(2,1)}, bf16[320,1120]{1,0:T(8,128)(2,1)}, bf16[1152,1120]{1,0:T(8,128)(2,1)}, bf16[1152,1120]{1,0:T(8,128)(2,1)}, bf16[1152,1120]{1,0:T(8,128)(2,1)}, /*index=5*/f32[16,1120]{1,0:T(8,128)}) custom-call(bf16[1280,280]{1,0:T(8,128)(2,1)} %get-tuple-element.79.dq, bf16[1280,280]{1,0:T(8,128)(2,1)} %get-tuple-element.83.dk, ...), custom_call_target="tpu_custom_call" | custom-call | tf_op jit(solution)/shard_map/exit/pallas_call | solution.py:1119
  380.7 0.0 copy-start.7
  380.8 3.8 convert_bitcast_fusion
  384.6 2.2 fusion.6
  386.8 2.7 slice_convert_fusion
  389.5 0.2 copy-done.6
  389.7 2.7 slice_convert_fusion.1
  392.4 1.7 slice_reduce_fusion
  394.1 0.7 dynamic-slice_reduce_fusion.1
  394.8 0.7 reshape_squeeze.3
  395.5 0.9 copy.39
  396.3 0.9 copy.40
  (25 shorter events, 0.1 us)
Async XLA Ops:
  0.6 4.4 %slice-start = ((bf16[1120,1120]{1,0:T(8,128)(2,1)}), bf16[32,1120]{1,0:T(8,128)(2,1)S(1)}, s32[]{:S(2)}) async-start(bf16[1120,1120]{1,0:T(8,128)(2,1)} %wu.1), calls=%async_computation | async-start | bytes 147456 | tf_op jit(solution)/shard_map/slice | solution.py:1165
  0.7 4.4 %slice-start.1 = ((bf16[1120,1120]{1,0:T(8,128)(2,1)}), bf16[32,1120]{1,0:T(8,128)(2,1)S(1)}, s32[]{:S(2)}) async-start(bf16[1120,1120]{1,0:T(8,128)(2,1)} %wd.1), calls=%async_computation.1 | async-start | bytes 147456 | tf_op jit(solution)/shard_map/slice | solution.py:1165
  78.5 33.2 %collective-permute-start = (bf16[608,1120]{1,0:T(8,128)(2,1)S(1)}, bf16[608,1120]{1,0:T(8,128)(2,1)S(1)}, u32[]{:S(2)}, u32[]{:S(2)}) collective-permute-start(bf16[608,1120]{1,0:T(8,128)(2,1)S(1)} %pad_maximum_fusion), channel_id=1, source_target_pairs={{0,2},{1,3},{6,4},{7,5},{8,10},{9,11},{14,12},{15,13},{16,18},{17,... | collective-permute-start | bytes 4085768 | tf_op jit(solution)/shard_map/ppermute | solution.py:1168
  79.8 31.9 %collective-permute-start.1 = (bf16[320,1120]{1,0:T(8,128)(2,1)}, bf16[320,1120]{1,0:T(8,128)(2,1)}, u32[]{:S(2)}, u32[]{:S(2)}) collective-permute-start(bf16[320,1120]{1,0:T(8,128)(2,1)} %get-tuple-element.65.cot_own), channel_id=1, source_target_pairs={{0,1},{1,0},{2,3},{3,2},{4,5},{5,4},{6,7},{7,6},{8,9},{9,8},{10,11... | collective-permute-start | bytes 2150408 | tf_op jit(solution)/shard_map/ppermute | solution.py:1167
  111.7 1.1 copy-start.8
  112.8 50.6 %copy-start.16 = (f32[1120]{0:T(1024)S(1)}, f32[1120]{0:T(1024)}, u32[]{:S(2)}) copy-start(f32[1120]{0:T(1024)} %get-tuple-element.70) | copy-start | bytes 13444
  163.4 7.7 %copy-start.2 = (bf16[1280,1120]{1,0:T(8,128)(2,1)S(1)}, bf16[1280,1120]{1,0:T(8,128)(2,1)}, u32[]{:S(2)}) copy-start(bf16[1280,1120]{1,0:T(8,128)(2,1)} %get-tuple-element.66.cot_full) | copy-start | bytes 8601604
  171.1 5.5 %copy-start.3 = (bf16[1280,1120]{1,0:T(8,128)(2,1)}, bf16[1280,1120]{1,0:T(8,128)(2,1)S(1)}, u32[]{:S(2)}) copy-start(bf16[1280,1120]{1,0:T(8,128)(2,1)S(1)} %get-tuple-element.107.act) | copy-start | bytes 8601604
  171.1 5.5 %copy-start.5 = (bf16[1120,1120]{1,0:T(8,128)(2,1)S(1)}, bf16[1120,1120]{1,0:T(8,128)(2,1)}, u32[]{:S(2)}) copy-start(bf16[1120,1120]{1,0:T(8,128)(2,1)} %get-tuple-element.67.wd) | copy-start | bytes 7526404
  176.6 9.0 %copy-start.15 = (bf16[1280,1120]{1,0:T(8,128)(2,1)S(1)}, bf16[1280,1120]{1,0:T(8,128)(2,1)}, u32[]{:S(2)}) copy-start(bf16[1280,1120]{1,0:T(8,128)(2,1)} %get-tuple-element.68) | copy-start | bytes 8601604
  185.6 5.5 %copy-start.4 = (bf16[1280,1120]{1,0:T(8,128)(2,1)}, bf16[1280,1120]{1,0:T(8,128)(2,1)S(1)}, u32[]{:S(2)}) copy-start(bf16[1280,1120]{1,0:T(8,128)(2,1)S(1)} %get-tuple-element.110.gi) | copy-start | bytes 8601604
  251.2 38.1 %collective-permute-start.3 = (bf16[576,1120]{1,0:T(8,128)(2,1)}, bf16[576,1120]{1,0:T(8,128)(2,1)S(1)}, u32[]{:S(2)}, u32[]{:S(2)}) collective-permute-start(bf16[576,1120]{1,0:T(8,128)(2,1)} %get-tuple-element.80.slices), channel_id=1, source_target_pairs={{2,0},{3,1},{4,6},{5,7},{10,8},{11,9},{12,14},{13,15},{18,16},{19,... | collective-permute-start | bytes 3870728 | tf_op jit(solution)/shard_map/ppermute | solution.py:1210
  254.5 32.6 %collective-permute-start.2 = (bf16[320,1120]{1,0:T(8,128)(2,1)}, bf16[320,1120]{1,0:T(8,128)(2,1)}, u32[]{:S(2)}, u32[]{:S(2)}) collective-permute-start(bf16[320,1120]{1,0:T(8,128)(2,1)} %get-tuple-element.72), channel_id=1, source_target_pairs={{0,1},{1,0},{2,3},{3,2},{4,5},{5,4},{6,7},{7,6},{8,9},{9,8},{10,11... | collective-permute-start | bytes 2150408 | tf_op jit(solution)/shard_map/ppermute | solution.py:1211
  255.3 24.7 %copy-start.11 = (bf16[1280,280]{1,0:T(8,128)(2,1)S(1)}, bf16[1280,280]{1,0:T(8,128)(2,1)}, u32[]{:S(2)}) copy-start(bf16[1280,280]{1,0:T(8,128)(2,1)} %get-tuple-element.61.att.o) | copy-start | bytes 2150404
  280.0 7.0 %copy-start = (bf16[1280,280]{1,0:T(8,128)(2,1)S(1)}, bf16[1280,280]{1,0:T(8,128)(2,1)}, u32[]{:S(2)}) copy-start(bf16[1280,280]{1,0:T(8,128)(2,1)} %get-tuple-element.79.dq) | copy-start | bytes 2150404
  280.0 7.2 %copy-start.14 = (bf16[1280,1120]{1,0:T(8,128)(2,1)S(1)}, bf16[1280,1120]{1,0:T(8,128)(2,1)}, u32[]{:S(2)}) copy-start(bf16[1280,1120]{1,0:T(8,128)(2,1)} %get-tuple-element.58.normed) | copy-start | bytes 8601604
  287.3 2.0 copy-start.1
  289.3 2.2 copy-start.9
  289.5 2.0 copy-start.10
  380.7 6.1 %copy-start.7 = (bf16[1152,1120]{1,0:T(8,128)(2,1)S(1)}, bf16[1152,1120]{1,0:T(8,128)(2,1)}, u32[]{:S(2)}) copy-start(bf16[1152,1120]{1,0:T(8,128)(2,1)} %get-tuple-element.95) | copy-start | bytes 7741444
  386.8 2.9 copy-start.6
  389.7 5.8 %copy-start.13 = (bf16[320,1120]{1,0:T(8,128)(2,1)S(1)}, bf16[320,1120]{1,0:T(8,128)(2,1)}, u32[]{:S(2)}) copy-start(bf16[320,1120]{1,0:T(8,128)(2,1)} %get-tuple-element.90) | copy-start | bytes 2150404
  389.7 6.7 %copy-start.12 = (bf16[320,1120]{1,0:T(8,128)(2,1)S(1)}, bf16[320,1120]{1,0:T(8,128)(2,1)}, u32[]{:S(2)}) copy-start(bf16[320,1120]{1,0:T(8,128)(2,1)} %get-tuple-element.91) | copy-start | bytes 2150404
where the time goes:
time: 403 us; the launch traced here: 398 us
  Pallas kernels  317 us (79%)
  matrix products  37.6 us (9%)
  other arithmetic  14.2 us (4%)
  waiting for transfers between devices  11.4 us (3%)
  local copies, waits for them, and re-layouts  11.1 us (3%)
  starting transfers between devices  4.73 us (1%)
    pallas_call x1, Pallas kernels, make_exit(): call(dq, dk, dv, wq, own, gmid, slices, far, res, res_near, *grads, small...  85.8 us
    pallas_call x1, Pallas kernels, enter(): return call(hid, cot, ids, qv, ub, wq, wo, *vecs)  73.3 us
    pallas_call x1, Pallas kernels, make_back(): return call(gi, wu, act, wd, grads_u, grads_d, mid, cot, *vecs)  60.1 us
    pallas_call x1, Pallas kernels, make_mid(): return call(att, wo, own, *vecs, wu, wd, pieces, cot_own, cot_near)  50.6 us
    pallas_call x1, Pallas kernels, attn_bwd(): pl.pallas_call(functools.partial(attn_bwd_kernel, heads, shard), out_shap...  24.7 us
    pallas_call x1, Pallas kernels, attn_fwd(): pl.pallas_call(functools.partial(attn_fwd_kernel, heads, shard), out_shap...  22.1 us
    dot_general x6, matrix products, mm_tn(): lax.dot_general(a, b, (((0,), (0,)), ((), ())), preferred_element_type=F32)  20.9 us
    dot_general x1, matrix products, mm_nt(): lax.dot_general(a, b, (((1,), (1,)), ((), ())), preferred_element_type=F32)  8.95 us
  transfers between devices with their start and end apart: 4, of which 2 were waited for; matrix products, arithmetic and copies ran while one was open for 2% of the time, Pallas kernels for 12%

commit v1 on v0

--- a/solution.py
+++ b/solution.py
@@ -469,11 +469,8 @@
         self.at = pl.multiple_of(lax.div(place.d, 2) * self.unit, 16)
         self.pieces, self.shared = [], []
 
-    def cut(self, ref, at, count):
-        return ref.at[:, pl.ds(at, count)] if len(ref.shape) == 3 else ref.at[pl.ds(at, count)]
-
     def move(self, src, at, count, to, when):
-        return self.link.send(self.cut(src, at, count), self.cut(self.dst, at, count), to, when)
+        return self.link.send(rows_of(src, at, count), rows_of(self.dst, at, count), to, when)
 
     def open(self):
         far, home = self.place.far, self.place.home
@@ -566,11 +563,13 @@
         src, base = (self.source, self.first) if s == 0 else (self.work[s - 1], 0)
         self.copies[s].wait_recv()
 
-        @pl.loop(0, n // 16)
+        step = step_of(n)
+
+        @pl.loop(0, n // step)
         def _(r):
-            here = pl.multiple_of(base + bit * n + r * 16, 16)
-            to = pl.ds(pl.multiple_of(r * 16, 16), 16)
-            total = src[pl.ds(here, 16), :].astype(F32) + self.got[s][to, :].astype(F32)
+            here = pl.multiple_of(base + bit * n + r * step, 16)
+            to = pl.ds(pl.multiple_of(r * step, 16), step)
+            total = src[pl.ds(here, step), :].astype(F32) + self.got[s][to, :].astype(F32)
             self.work[s][to, :] = total.astype(BF)
 
     def offset(self):
@@ -579,6 +578,16 @@
             n //= 2
             at = at + self.place.bit(b) * n
         return self.first + at
+
+
+def step_of(n):
+    return next(step for step in (48, 32, 16) if n % step == 0)
+
+
+def groups_of(side, unit):
+    units = side // unit
+    first = max(1, min(units - 1, 2 * units // 3))
+    return [count * unit for count in (first, units - first) if count]
 
 
 def halving_scratch(size, bits, model):
@@ -610,10 +619,12 @@
 
         @pl.when(self.place.home)
         def _():
-            @pl.loop(0, self.n // 16)
+            step = step_of(self.n)
+
+            @pl.loop(0, self.n // step)
             def _(r):
-                here = pl.ds(pl.multiple_of(r * 16, 16), 16)
-                to = pl.ds(pl.multiple_of(self.at + r * 16, 16), 16)
+                here = pl.ds(pl.multiple_of(r * step, 16), step)
+                to = pl.ds(pl.multiple_of(self.at + r * step, 16), step)
                 total = self.slice_ref[here, :].astype(F32) + self.far_buf[here, :].astype(F32)
                 self.full[to, :] = total.astype(BF)
 
@@ -672,7 +683,8 @@
     n = shard // CHUNKS
     home, away = place.home, place.away
     meet([place.core, place.near, place.far, place.swap] + [place.column(m) for m in range(1, columns)])
-    weights = [Spread(link, place, wq, wq_o), Spread(link, place, wo, wo_o)]
+    weights = [Spread(link, place, wq.at[j], wq_o.at[j]) for j in range(wq.shape[0])]
+    weights.append(Spread(link, place, wo, wo_o))
 
     ids_copy = link.send(ids, ids_o, place.swap, away)
     swaps = [
@@ -890,10 +902,10 @@
     inp, out, full_u, full_d, full_a, small = refs[:6]
     scratch = list(refs[6:-3])
     a_bufs = scratch[:4]
-    swap_buf, out_buf, far_a0, far_a1, grads_a = scratch[4:9]
+    swap_buf, out_buf, grads_a = scratch[4:7]
     steps = bits + 3
-    sum_own, sum_got = scratch[9 : 9 + steps], scratch[9 + steps : 9 + 2 * steps]
-    halves = scratch[9 + 2 * steps :]
+    sum_own, sum_got = scratch[7 : 7 + steps], scratch[7 + steps : 7 + 2 * steps]
+    halves = scratch[7 + 2 * steps :]
     n = shard // CHUNKS
     local = Local(refs[-1])
     pack(local, [gq, gk, gv, go], grads_a)
@@ -905,52 +917,55 @@
         return mm(dq[rows, :], wq[0]) + mm(dk[rows, :], wq[1]) + mm(dv[rows, :], wq[2])
 
     total = Scatter(link, place, make, *a_bufs, shard)
-    half_a = []
-    for side in range(2):
-        half_a.append(
-            Halving(
-                link, place, grads_a, side * (size // 2), size // 2, side,
+    groups, at = [], 0
+    for count in groups_of(size // 2, 16 * columns):
+        group = []
+        for side in range(2):
+            half = Halving(
+                link, place, grads_a, side * (size // 2) + at, count, side,
                 halves[:bits], halves[bits : 2 * bits],
             )
-        )
-        halves = halves[2 * bits :]
+            group.append(Doubling(link, place, half, full_a, half.work[bits - 1], halves[2 * bits]))
+            halves = halves[2 * bits + 1 :]
+        groups.append(group)
+        at += count
     half_u = Halving(link, place, None, 0, size, 0, [], [])
     half_d = Halving(link, place, None, 0, size, 1, [], [])
     held = size // columns
     double = [
         Doubling(link, place, half_u, full_u, rows_of(slices, 0, held), rows_of(far, 0, held)),
         Doubling(link, place, half_d, full_d, rows_of(slices, held, held), rows_of(far, held, held)),
-        Doubling(link, place, half_a[0], full_a, half_a[0].work[bits - 1], far_a0),
-        Doubling(link, place, half_a[1], full_a, half_a[1].work[bits - 1], far_a1),
     ]
     local.drain()
-    half_a[0].start(0)
-    half_a[1].start(0)
+    for group in groups:
+        for one in group:
+            one.half.start(0)
+
+    def finish_out(here):
+        value = (res[here, :] + res_near[here, :].astype(F32)).astype(BF)
+        out_buf[here, :] = value
+
+        @pl.when(place.home)
+        def _():
+            out[here, :] = value
+
+    over_rows(0, shard, STEP, finish_out)
+    swaps = [link.send(out_buf, out, place.swap, place.away)]
     total.start()
     for i in range(CHUNKS):
         total.pass_on(i)
     total.rest()
-
-    def finish_out(here):
-        value = (res[here, :] + res_near[here, :].astype(F32)).astype(BF)
-        out_buf[here, :] = value
-
-        @pl.when(place.home)
-        def _():
-            out[here, :] = value
-
-    over_rows(0, shard, STEP, finish_out)
-    swaps = [link.send(out_buf, out, place.swap, place.away)]
     sum_own[0][...] = small_in[...]
     for s in range(bits):
-        for half in half_a:
-            half.finish(s)
-            if s + 1 < bits:
-                half.start(s + 1)
-    double[2].start()
-    double[3].start()
-    double[0].join()
-    double[1].join()
+        for group in groups:
+            for one in group:
+                one.half.finish(s)
+                if s + 1 < bits:
+                    one.half.start(s + 1)
+                else:
+                    one.start()
+    for one in double:
+        one.join()
     for i in range(CHUNKS):
         total.ready(i)
 
@@ -979,25 +994,19 @@
         if s + 1 < steps:
             hop_copies.append(link.send(sum_own[s + 1], sum_got[s + 1], hops[s + 1]))
 
+    chain = [one.join for one in groups[0]] + [None]
+    for s in range(bits):
+        chain += [one.advance for one in double] + [None] + [one.advance for one in groups[0]]
+        chain += [one.advance if s else one.join for group in groups[1:] for one in group] + [None]
+    chain += [one.advance for group in groups[1:] for one in group]
     hop = 0
-    for s in range(bits):
-        double[0].advance()
-        double[1].advance()
-        if s == 0:
-            double[2].join()
-            double[3].join()
-        else:
-            double[2].advance()
-            double[3].advance()
-        if hop < steps:
+    for act in chain + [None] * steps:
+        if act is not None:
+            act()
+        elif hop < steps:
             next_hop(hop)
             hop += 1
-    double[2].advance()
-    double[3].advance()
-    while hop < steps:
-        next_hop(hop)
-        hop += 1
-    for one in double:
+    for one in double + [one for group in groups for one in group]:
         for copy in one.cores:
             arrive(copy, place.away)
     for copy in swaps:
@@ -1099,8 +1108,10 @@
         shaped((size, model), BF),
         shaped(small.shape, F32),
     )
-    n = size // columns
-    per_side = halving_scratch(size // 2, bits, model)
+    halves = []
+    for count in groups_of(size // 2, 16 * columns):
+        per_side = halving_scratch(count, bits, model)
+        halves += (per_side + per_side + [per_side[-1]]) * 2
     steps = bits + 3
     call = remote_call(
         "exit", functools.partial(exit_kernel, columns, shard), 3, outs,
@@ -1109,12 +1120,10 @@
         + [
             pltpu.VMEM((shard, model), BF),
             pltpu.VMEM((shard, model), BF),
-            pltpu.VMEM((n // 2, model), BF),
-            pltpu.VMEM((n // 2, model), BF),
             pltpu.VMEM((size, model), BF),
         ]
         + [pltpu.VMEM(small.shape, F32)] * (2 * steps)
-        + (per_side + per_side) * 2,
+        + halves,
     )
     return call(dq, dk, dv, wq, own, gmid, slices, far, res, res_near, *grads, small, vec)
 

time: 403 us -> 407 us (level)
  no operation moved by 1% of the time
where the time goes in v1:
time: 407 us; the launch traced here: 401 us
  Pallas kernels  320 us (79%)
  matrix products  37.7 us (9%)
  other arithmetic  14.2 us (3%)
  waiting for transfers between devices  11.6 us (3%)
  local copies, waits for them, and re-layouts  11.1 us (3%)
  starting transfers between devices  4.75 us (1%)
    pallas_call x1, Pallas kernels, make_exit(): call(dq, dk, dv, wq, own, gmid, slices, far, res, res_near, *grads, small...  89 us
    pallas_call x1, Pallas kernels, enter(): return call(hid, cot, ids, qv, ub, wq, wo, *vecs)  73.4 us
    pallas_call x1, Pallas kernels, make_back(): return call(gi, wu, act, wd, grads_u, grads_d, mid, cot, *vecs)  59.7 us
    pallas_call x1, Pallas kernels, make_mid(): return call(att, wo, own, *vecs, wu, wd, pieces, cot_own, cot_near)  50.6 us
    pallas_call x1, Pallas kernels, attn_bwd(): pl.pallas_call(functools.partial(attn_bwd_kernel, heads, shard), out_shap...  24.6 us
    pallas_call x1, Pallas kernels, attn_fwd(): pl.pallas_call(functools.partial(attn_fwd_kernel, heads, shard), out_shap...  22.1 us
    dot_general x6, matrix products, mm_tn(): lax.dot_general(a, b, (((0,), (0,)), ((), ())), preferred_element_type=F32)  20.9 us
    dot_general x1, matrix products, mm_nt(): lax.dot_general(a, b, (((1,), (1,)), ((), ())), preferred_element_type=F32)  9.14 us
  transfers between devices with their start and end apart: 4, of which 2 were waited for; matrix products, arithmetic and copies ran while one was open for 2% of the time, Pallas kernels for 12%

profile of v1, /device:TPU:1, one launch (start us, length us, event | category | flops | bytes accessed | tf_op | source)
XLA Modules:
  0.0 400.6 jit_solution(11070720294817304887)
XLA Ops:
  0.6 0.0 slice-start
  0.7 0.0 slice-start.1
  0.7 1.4 constant_dynamic-slice_fusion
  2.7 0.7 fusion.8
  3.5 0.8 convert_reduce_fusion
  4.3 0.1 slice.48
  4.4 0.1 concatenate.15
  4.5 0.6 broadcast_in_dim.51.ids
  5.1 0.0 slice-done
  5.1 0.0 slice-done.1
  5.1 0.1 pad_maximum_fusion
  5.2 73.4 %enter.1 = (bf16[320,1120]{1,0:T(8,128)(2,1)}, bf16[1280,1120]{1,0:T(8,128)(2,1)}, bf16[320,1120]{1,0:T(8,128)(2,1)}, s32[1,1408]{1,0:T(1,128)}, f32[2,280]{1,0:...) custom-call(bf16[320,1120]{1,0:T(8,128)(2,1)} %bitcast.38, ...), custom_call_target="tpu_custom_call" | custom-call | tf_op jit(solution)/shard_map/enter/pallas_call | solution.py:1060
  78.6 1.3 collective-permute-start
  79.9 0.1 collective-permute-start.1
  80.0 0.7 slice_bitcast_fusion.1
  80.7 0.6 pad_add_fusion.meta
  81.2 22.1 %attn_fwd.1 = (bf16[1280,280]{1,0:T(8,128)(2,1)}, f32[8,1280]{1,0:T(8,128)}, bf16[1280,384]{1,0:T(8,128)(2,1)}, bf16[1280,384]{1,0:T(8,128)(2,1)}, bf16[1280,384]{1,0:T(8,128)(2,1)}) custom-call(s32[6]{0:T(128)} %pad_add_fusion.meta, s32[1,1408]{1,0:T(1,128)} %get-tuple-element.55.start, bf16[1280,1120]{1,0:T(8,128)(2,1)} %get-tuple-element.58.normed, ...), custom_call_target="tpu_custom_call" | custom-call | flops 1376256000 | bytes 5734400 | tf_op jit(solution)/shard_map/attn_fwd/pallas_call | solution.py:236
  103.4 8.4 %collective-permute-done.1.cot_near = bf16[320,1120]{1,0:T(8,128)(2,1)} collective-permute-done((bf16[320,1120]{1,0:T(8,128)(2,1)}, bf16[320,1120]{1,0:T(8,128)(2,1)}, u32[]{:S(2)}, u32[]{:S(2)}) %collective-permute-start.1) | collective-permute-done | bytes 716832 | tf_op jit(solution)/shard_map/ppermute | solution.py:1176
  111.8 0.0 collective-permute-done.pieces
  111.8 1.1 copy-done.8
  112.9 50.6 %mid.1 = (f32[320,1120]{1,0:T(8,128)}, bf16[1280,1120]{1,0:T(8,128)(2,1)}, bf16[1280,1120]{1,0:T(8,128)(2,1)}, bf16[1120,1120]{1,0:T(8,128)(2,1)}, bf16[1120,1120]{1,0:T(8,128)(2,1)}) custom-call(bf16[1280,280]{1,0:T(8,128)(2,1)} %get-tuple-element.61.att.o, bf16[280,1120]{1,0:T(8,128)(2,1)} %get-tuple-element.62.wo, ...), custom_call_target="tpu_custom_call" | custom-call | tf_op jit(solution)/shard_map/mid/pallas_call | solution.py:1071
  163.5 0.0 copy-done.16
  163.5 0.0 copy-start.2
  163.5 7.7 %multiply_convert_fusion = (bf16[1280,1120]{1,0:T(8,128)(2,1)S(1)}, f32[1280,1120]{1,0:T(8,128)S(1)}) fusion(f32[1120]{0:T(1024)S(1)} %copy-done.16, bf16[1280,1120]{1,0:T(8,128)(2,1)} %get-tuple-element.68, bf16[1120,1120]{1,0:T(8,128)(2,1)} %get-tuple-element.69.wu), kind=kOutput, calls=%fused_computation.14 | convolution fusion | flops 3225600000 | bytes 13982080 | tf_op jit(solution)/shard_map/dot_general | solution.py:20
  171.2 0.0 copy-start.3
  171.2 0.0 copy-done.2
  171.2 0.0 copy-start.5
  171.2 5.5 %convolution_convert_fusion.raw_d = bf16[1120,1120]{1,0:T(8,128)(2,1)} fusion(bf16[1280,1120]{1,0:T(8,128)(2,1)S(1)} %get-tuple-element.107.act, bf16[1280,1120]{1,0:T(8,128)(2,1)S(1)} %copy-done.2), kind=kOutput, calls=%fused_computation.4 | convolution fusion | flops 3212518400 | bytes 8243200 | tf_op jit(solution)/shard_map/dot_general | solution.py:28
  176.7 0.0 copy-done.3
  176.7 0.0 copy-done.5
  176.7 9.1 %convert_reduce_fusion.1 = (f32[1120]{0:T(1024)S(1)}, bf16[1280,1120]{1,0:T(8,128)(2,1)S(1)}) fusion(f32[1280,1120]{1,0:T(8,128)S(1)} %get-tuple-element.108, bf16[1280,1120]{1,0:T(8,128)(2,1)S(1)} %copy-done.2, bf16[1120,1120]{1,0:T(8,128)(2,1)S(1)} %copy-done.5), kind=kOutput, calls=%fused_computation.13 | convolution fusion | flops 3241368576 | bytes 13982080 | tf_op jit(solution)/shard_map/dot_general | solution.py:24
  185.9 0.0 copy-start.4
  185.9 0.0 copy-done.15
  185.9 5.5 %convolution_convert_fusion.1.raw_u = bf16[1120,1120]{1,0:T(8,128)(2,1)} fusion(bf16[1280,1120]{1,0:T(8,128)(2,1)S(1)} %copy-done.15, bf16[1280,1120]{1,0:T(8,128)(2,1)S(1)} %get-tuple-element.110.gi), kind=kOutput, calls=%fused_computation.5 | convolution fusion | flops 3212518400 | bytes 8243200 | tf_op jit(solution)/shard_map/dot_general | solution.py:28
  191.4 59.7 %back.1 = (f32[320,1120]{1,0:T(8,128)}, bf16[1280,1120]{1,0:T(8,128)(2,1)}, f32[320,1120]{1,0:T(8,128)}, bf16[320,1120]{1,0:T(8,128)(2,1)}, bf16[576,1120]{1,0:T(8,128)(2,1)}, /*index=5*/f32[8,1120]{1,0:T(8,128)}) custom-call(bf16[1280,1120]{1,0:T(8,128)(2,1)} %copy-done.4, bf16[1120,1120]{1,0:T(8,128)(2,1)} %get-tuple-element.69.wu, ...), custom_call_target="tpu_custom_call" | custom-call | tf_op jit(solution)/shard_map/back/pallas_call | solution.py:1097
  251.1 3.2 collective-permute-start.3
  254.3 0.2 collective-permute-start.2
  254.5 0.8 slice.52
  255.3 24.6 %attn_bwd.1 = (bf16[1280,280]{1,0:T(8,128)(2,1)}, bf16[1280,280]{1,0:T(8,128)(2,1)}, bf16[1280,280]{1,0:T(8,128)(2,1)}) custom-call(s32[6]{0:T(128)} %pad_add_fusion.meta, s32[1,1408]{1,0:T(1,128)} %get-tuple-element.55.start, bf16[1280,384]{1,0:T(8,128)(2,1)} %get-tuple-element.73.qs, bf16[1280,384]{1,0:T(8,128)(2,1)} %get-tuple-element.74.ks, ...), custom_call_target="tpu_custom_call" | custom-call | flops 3670016000 | bytes 5734400 | tf_op jit(solution)/shard_map/attn_bwd/pallas_call | solution.py:265
  279.9 0.0 copy-done.11
  279.9 4.0 convolution_convert_fusion.2.go
  283.9 3.2 collective-permute-done.2.res_near
  287.1 0.2 convert_reduce_fusion.3
  287.3 0.0 copy-done.14
  287.3 2.0 convolution_convert_fusion.5.gq
  289.3 0.0 collective-permute-done.3.far
  289.3 0.2 convert_reduce_fusion.2
  289.5 2.0 convolution_convert_fusion.3.gv
  291.5 2.0 convolution_convert_fusion.4.gk
  293.5 0.1 select_maximum_fusion
  293.6 0.1 broadcast_select_fusion
  293.7 1.3 concatenate.19.small_in
  294.9 89.0 %exit.1 = (bf16[320,1120]{1,0:T(8,128)(2,1)}, bf16[320,1120]{1,0:T(8,128)(2,1)}, bf16[1152,1120]{1,0:T(8,128)(2,1)}, bf16[1152,1120]{1,0:T(8,128)(2,1)}, bf16[1152,1120]{1,0:T(8,128)(2,1)}, /*index=5*/f32[16,1120]{1,0:T(8,128)}) custom-call(bf16[1280,280]{1,0:T(8,128)(2,1)} %get-tuple-element.79.dq, bf16[1280,280]{1,0:T(8,128)(2,1)} %get-tuple-element.83.dk, ...), custom_call_target="tpu_custom_call" | custom-call | tf_op jit(solution)/shard_map/exit/pallas_call | solution.py:1128
  384.0 0.0 copy-start.7
  384.0 3.8 convert_bitcast_fusion
  387.8 2.2 fusion.6
  390.1 2.7 slice_convert_fusion
  392.7 0.2 copy-done.6
  392.9 2.7 slice_convert_fusion.1
  395.6 1.7 slice_reduce_fusion
  397.3 0.7 dynamic-slice_reduce_fusion.1
  398.0 0.7 reshape_squeeze.3
  398.7 0.9 copy.39
  399.6 0.9 copy.40
  (25 shorter events, 0.1 us)
Async XLA Ops:
  0.6 4.4 %slice-start = ((bf16[1120,1120]{1,0:T(8,128)(2,1)}), bf16[32,1120]{1,0:T(8,128)(2,1)S(1)}, s32[]{:S(2)}) async-start(bf16[1120,1120]{1,0:T(8,128)(2,1)} %wu.1), calls=%async_computation | async-start | bytes 147456 | tf_op jit(solution)/shard_map/slice | solution.py:1174
  0.7 4.4 %slice-start.1 = ((bf16[1120,1120]{1,0:T(8,128)(2,1)}), bf16[32,1120]{1,0:T(8,128)(2,1)S(1)}, s32[]{:S(2)}) async-start(bf16[1120,1120]{1,0:T(8,128)(2,1)} %wd.1), calls=%async_computation.1 | async-start | bytes 147456 | tf_op jit(solution)/shard_map/slice | solution.py:1174
  78.6 33.2 %collective-permute-start = (bf16[608,1120]{1,0:T(8,128)(2,1)S(1)}, bf16[608,1120]{1,0:T(8,128)(2,1)S(1)}, u32[]{:S(2)}, u32[]{:S(2)}) collective-permute-start(bf16[608,1120]{1,0:T(8,128)(2,1)S(1)} %pad_maximum_fusion), channel_id=1, source_target_pairs={{0,2},{1,3},{6,4},{7,5},{8,10},{9,11},{14,12},{15,13},{16,18},{17,... | collective-permute-start | bytes 4085768 | tf_op jit(solution)/shard_map/ppermute | solution.py:1177
  79.9 31.9 %collective-permute-start.1 = (bf16[320,1120]{1,0:T(8,128)(2,1)}, bf16[320,1120]{1,0:T(8,128)(2,1)}, u32[]{:S(2)}, u32[]{:S(2)}) collective-permute-start(bf16[320,1120]{1,0:T(8,128)(2,1)} %get-tuple-element.65.cot_own), channel_id=1, source_target_pairs={{0,1},{1,0},{2,3},{3,2},{4,5},{5,4},{6,7},{7,6},{8,9},{9,8},{10,11... | collective-permute-start | bytes 2150408 | tf_op jit(solution)/shard_map/ppermute | solution.py:1176
  111.8 1.1 copy-start.8
  112.9 50.6 %copy-start.16 = (f32[1120]{0:T(1024)S(1)}, f32[1120]{0:T(1024)}, u32[]{:S(2)}) copy-start(f32[1120]{0:T(1024)} %get-tuple-element.70) | copy-start | bytes 13444
  163.5 7.7 %copy-start.2 = (bf16[1280,1120]{1,0:T(8,128)(2,1)S(1)}, bf16[1280,1120]{1,0:T(8,128)(2,1)}, u32[]{:S(2)}) copy-start(bf16[1280,1120]{1,0:T(8,128)(2,1)} %get-tuple-element.66.cot_full) | copy-start | bytes 8601604
  171.2 5.5 %copy-start.3 = (bf16[1280,1120]{1,0:T(8,128)(2,1)}, bf16[1280,1120]{1,0:T(8,128)(2,1)S(1)}, u32[]{:S(2)}) copy-start(bf16[1280,1120]{1,0:T(8,128)(2,1)S(1)} %get-tuple-element.107.act) | copy-start | bytes 8601604
  171.2 5.5 %copy-start.5 = (bf16[1120,1120]{1,0:T(8,128)(2,1)S(1)}, bf16[1120,1120]{1,0:T(8,128)(2,1)}, u32[]{:S(2)}) copy-start(bf16[1120,1120]{1,0:T(8,128)(2,1)} %get-tuple-element.67.wd) | copy-start | bytes 7526404
  176.7 9.2 %copy-start.15 = (bf16[1280,1120]{1,0:T(8,128)(2,1)S(1)}, bf16[1280,1120]{1,0:T(8,128)(2,1)}, u32[]{:S(2)}) copy-start(bf16[1280,1120]{1,0:T(8,128)(2,1)} %get-tuple-element.68) | copy-start | bytes 8601604
  185.9 5.5 %copy-start.4 = (bf16[1280,1120]{1,0:T(8,128)(2,1)}, bf16[1280,1120]{1,0:T(8,128)(2,1)S(1)}, u32[]{:S(2)}) copy-start(bf16[1280,1120]{1,0:T(8,128)(2,1)S(1)} %get-tuple-element.110.gi) | copy-start | bytes 8601604
  251.1 38.2 %collective-permute-start.3 = (bf16[576,1120]{1,0:T(8,128)(2,1)}, bf16[576,1120]{1,0:T(8,128)(2,1)S(1)}, u32[]{:S(2)}, u32[]{:S(2)}) collective-permute-start(bf16[576,1120]{1,0:T(8,128)(2,1)} %get-tuple-element.80.slices), channel_id=1, source_target_pairs={{2,0},{3,1},{4,6},{5,7},{10,8},{11,9},{12,14},{13,15},{18,16},{19,... | collective-permute-start | bytes 3870728 | tf_op jit(solution)/shard_map/ppermute | solution.py:1219
  254.3 32.7 %collective-permute-start.2 = (bf16[320,1120]{1,0:T(8,128)(2,1)}, bf16[320,1120]{1,0:T(8,128)(2,1)}, u32[]{:S(2)}, u32[]{:S(2)}) collective-permute-start(bf16[320,1120]{1,0:T(8,128)(2,1)} %get-tuple-element.72), channel_id=1, source_target_pairs={{0,1},{1,0},{2,3},{3,2},{4,5},{5,4},{6,7},{7,6},{8,9},{9,8},{10,11... | collective-permute-start | bytes 2150408 | tf_op jit(solution)/shard_map/ppermute | solution.py:1220
  255.3 24.6 %copy-start.11 = (bf16[1280,280]{1,0:T(8,128)(2,1)S(1)}, bf16[1280,280]{1,0:T(8,128)(2,1)}, u32[]{:S(2)}) copy-start(bf16[1280,280]{1,0:T(8,128)(2,1)} %get-tuple-element.61.att.o) | copy-start | bytes 2150404
  279.9 7.2 %copy-start = (bf16[1280,280]{1,0:T(8,128)(2,1)S(1)}, bf16[1280,280]{1,0:T(8,128)(2,1)}, u32[]{:S(2)}) copy-start(bf16[1280,280]{1,0:T(8,128)(2,1)} %get-tuple-element.79.dq) | copy-start | bytes 2150404
  279.9 7.4 %copy-start.14 = (bf16[1280,1120]{1,0:T(8,128)(2,1)S(1)}, bf16[1280,1120]{1,0:T(8,128)(2,1)}, u32[]{:S(2)}) copy-start(bf16[1280,1120]{1,0:T(8,128)(2,1)} %get-tuple-element.58.normed) | copy-start | bytes 8601604
  287.3 2.0 copy-start.1
  289.3 2.2 copy-start.9
  289.5 2.0 copy-start.10
  384.0 6.1 %copy-start.7 = (bf16[1152,1120]{1,0:T(8,128)(2,1)S(1)}, bf16[1152,1120]{1,0:T(8,128)(2,1)}, u32[]{:S(2)}) copy-start(bf16[1152,1120]{1,0:T(8,128)(2,1)} %get-tuple-element.95) | copy-start | bytes 7741444
  390.0 2.9 copy-start.6
  392.9 5.8 %copy-start.13 = (bf16[320,1120]{1,0:T(8,128)(2,1)S(1)}, bf16[320,1120]{1,0:T(8,128)(2,1)}, u32[]{:S(2)}) copy-start(bf16[320,1120]{1,0:T(8,128)(2,1)} %get-tuple-element.90) | copy-start | bytes 2150404
  392.9 6.7 %copy-start.12 = (bf16[320,1120]{1,0:T(8,128)(2,1)S(1)}, bf16[320,1120]{1,0:T(8,128)(2,1)}, u32[]{:S(2)}) copy-start(bf16[320,1120]{1,0:T(8,128)(2,1)} %get-tuple-element.91) | copy-start | bytes 2150404

commit v2 on v1

--- a/solution.py
+++ b/solution.py
@@ -732,12 +732,13 @@
 
 def mid_kernel(
     columns, shard, att, wo, own, bias, gain, shift, wu, wd, pieces, cot_own, cot_near,
-    mid, full, cfull, wu_o, wd_o,
+    mid, full_out, cfull_out, wu_out, wd_out, full, cfull, wu_o, wd_o,
     part, core_buf, out_buf, near_buf, send_sems, recv_sems, local_sems
 ):
     place, link = Place(columns), Link(send_sems, recv_sems)
     n = shard // CHUNKS
     home, away = place.home, place.away
+    stores = Local(local_sems, None, 8)
     unit, rest = pieces_of(wu, columns)
     at = pl.multiple_of(lax.div(place.d, 2) * unit, 16)
     mine = Local(local_sems, home, 0)
@@ -785,14 +786,22 @@
         over_rows(i * n, n, STEP, rows)
         near[i], copy = gather_start(link, place, full, shard, i)
         core.append(copy)
-    for i in range(CHUNKS):
-        core.append(gather_relay(link, place, full, shard, i, near[i]))
-    for copy in core:
-        copy.wait_recv()
     for copy in shared:
         arrive(copy, away)
     for local in (mine, both, other):
         local.drain()
+    for copy in core[:2]:
+        copy.wait_recv()
+    stores.keep(wu_o, wu_out)
+    stores.keep(wd_o, wd_out)
+    stores.keep(cfull, cfull_out)
+    for i in range(CHUNKS):
+        core.append(gather_relay(link, place, full, shard, i, near[i]))
+    stores.keep(rows_of(full, 0, 2 * shard), rows_of(full_out, 0, 2 * shard))
+    for copy in core[2:]:
+        copy.wait_recv()
+    stores.keep(rows_of(full, 2 * shard, 2 * shard), rows_of(full_out, 2 * shard, 2 * shard))
+    stores.drain()
     link.close()
 
 
@@ -895,12 +904,14 @@
 
 
 def exit_kernel(
-    columns, shard, dq, dk, dv, wq, own, gmid, slices, far, res, res_near, gq, gk, gv, go, small_in, gain, *refs
+    columns, shard, *refs
 ):
     place, link = Place(columns), Link(*refs[-3:-1])
     bits = place.bits
-    inp, out, full_u, full_d, full_a, small = refs[:6]
-    scratch = list(refs[6:-3])
+    given, (gq, gk, gv, go, small_in, gain), refs = refs[:10], refs[10:16], refs[16:]
+    inp, out, out_u, out_d, out_a, small = refs[:6]
+    held, (full_u, full_d, full_a), scratch = refs[6:16], refs[16:19], list(refs[19:-3])
+    res, res_near, dq, dk, dv, wq, slices, far, gmid, own = held
     a_bufs = scratch[:4]
     swap_buf, out_buf, grads_a = scratch[4:7]
     steps = bits + 3
@@ -909,6 +920,10 @@
     n = shard // CHUNKS
     local = Local(refs[-1])
     pack(local, [gq, gk, gv, go], grads_a)
+    loads = Local(refs[-1], None, 4)
+    for src, dst in zip(given, held):
+        loads.keep(src, dst)
+    stores = Local(refs[-1], None, 14)
     hops = [place.core] + [place.column(1 << b) for b in range(bits)] + [place.near, place.far]
     meet(hops + [place.swap])
     size = full_u.shape[0]
@@ -931,10 +946,10 @@
         at += count
     half_u = Halving(link, place, None, 0, size, 0, [], [])
     half_d = Halving(link, place, None, 0, size, 1, [], [])
-    held = size // columns
+    part = size // columns
     double = [
-        Doubling(link, place, half_u, full_u, rows_of(slices, 0, held), rows_of(far, 0, held)),
-        Doubling(link, place, half_d, full_d, rows_of(slices, held, held), rows_of(far, held, held)),
+        Doubling(link, place, half_u, full_u, rows_of(slices, 0, part), rows_of(far, 0, part)),
+        Doubling(link, place, half_d, full_d, rows_of(slices, part, part), rows_of(far, part, part)),
     ]
     local.drain()
     for group in groups:
@@ -949,8 +964,12 @@
         def _():
             out[here, :] = value
 
+    for copy in loads.copies[:2]:
+        copy.wait()
     over_rows(0, shard, STEP, finish_out)
     swaps = [link.send(out_buf, out, place.swap, place.away)]
+    for copy in loads.copies[2:6]:
+        copy.wait()
     total.start()
     for i in range(CHUNKS):
         total.pass_on(i)
@@ -964,6 +983,8 @@
                     one.half.start(s + 1)
                 else:
                     one.start()
+    for copy in loads.copies[6:]:
+        copy.wait()
     for one in double:
         one.join()
     for i in range(CHUNKS):
@@ -999,6 +1020,16 @@
         chain += [one.advance for one in double] + [None] + [one.advance for one in groups[0]]
         chain += [one.advance if s else one.join for group in groups[1:] for one in group] + [None]
     chain += [one.advance for group in groups[1:] for one in group]
+
+    def put(some, src, dst):
+        for one in some:
+            for copy in one.cores:
+                arrive(copy, place.away)
+        stores.keep(src, dst)
+
+    last = len(chain) - 1 - chain[::-1].index(double[1].advance)
+    chain.insert(last + 2, lambda: put(double[1:], full_d, out_d))
+    chain.insert(last + 2, lambda: put(double[:1], full_u, out_u))
     hop = 0
     for act in chain + [None] * steps:
         if act is not None:
@@ -1006,11 +1037,10 @@
         elif hop < steps:
             next_hop(hop)
             hop += 1
-    for one in double + [one for group in groups for one in group]:
-        for copy in one.cores:
-            arrive(copy, place.away)
+    put([one for group in groups for one in group], full_a, out_a)
     for copy in swaps:
         arrive(copy, place.away)
+    stores.drain()
     link.close()
 
 
@@ -1021,7 +1051,7 @@
 SEMS = 160
 
 
-def sems(local=8):
+def sems(local=24):
     return [
         pltpu.SemaphoreType.DMA((SEMS,)),
         pltpu.SemaphoreType.DMA((SEMS,)),
@@ -1029,18 +1059,22 @@
     ]
 
 
-def remote_call(name, kernel, number, outs, in_specs, scratch):
+def remote_call(name, kernel, number, outs, in_specs, scratch, away=()):
     return pl.pallas_call(
         kernel,
         out_shape=outs,
         in_specs=in_specs,
-        out_specs=jax.tree.map(lambda _: vmem(), outs),
+        out_specs=tuple(any_space() if j in away else vmem() for j in range(len(outs))),
         scratch_shapes=scratch + sems(),
         compiler_params=pltpu.CompilerParams(
             collective_id=number, has_side_effects=True, vmem_limit_bytes=62 << 20
         ),
         name=name,
     )
+
+
+def held_like(arrays):
+    return [pltpu.VMEM(x.shape, x.dtype) for x in arrays]
 
 
 def shaped(shape, dtype):
@@ -1066,7 +1100,8 @@
     outs = (shaped((shard, model), F32), whole, whole, like(wu), like(wd))
     call = remote_call(
         "mid", functools.partial(mid_kernel, columns, shard), 1, outs, [vmem()] * 6 + [any_space()] * 5,
-        scatter_scratch(shard, model),
+        held_like(outs[1:]) + scatter_scratch(shard, model),
+        away=(1, 2, 3, 4),
     )
     return call(att, wo, own, *vecs, wu, wd, pieces, cot_own, cot_near)
 
@@ -1099,6 +1134,7 @@
 
 def make_exit(columns, size, dq, dk, dv, wq, own, gmid, slices, far, res, res_near, grads, small, vec):
     shard, model = own.shape
+    given = (res, res_near, dq, dk, dv, wq, slices, far, gmid, own)
     bits = columns.bit_length() - 1
     outs = (
         shaped((shard, model), BF),
@@ -1115,8 +1151,10 @@
     steps = bits + 3
     call = remote_call(
         "exit", functools.partial(exit_kernel, columns, shard), 3, outs,
-        [vmem()] * 10 + [any_space()] * 4 + [vmem()] * 2,
-        scatter_scratch(shard, model)
+        [any_space()] * 14 + [vmem()] * 2,
+        held_like(given)
+        + [pltpu.VMEM((size, model), BF)] * 3
+        + scatter_scratch(shard, model)
         + [
             pltpu.VMEM((shard, model), BF),
             pltpu.VMEM((shard, model), BF),
@@ -1124,8 +1162,9 @@
         ]
         + [pltpu.VMEM(small.shape, F32)] * (2 * steps)
         + halves,
-    )
-    return call(dq, dk, dv, wq, own, gmid, slices, far, res, res_near, *grads, small, vec)
+        away=(2, 3, 4),
+    )
+    return call(*given, *grads, small, vec)
 
 
 def body(

time: 407 us -> 400 us (0.983)
  Pallas kernels: 320 us -> 313 us
    pallas_call x1, Pallas kernels: 89 us -> 84.2 us  [make_exit(): return call(*given, *grads, small, vec)]
where the time goes in v2:
time: 400 us; the launch traced here: 394 us
  Pallas kernels  313 us (78%)
  matrix products  37.7 us (9%)
  other arithmetic  14.2 us (4%)
  waiting for transfers between devices  11.5 us (3%)
  local copies, waits for them, and re-layouts  11.1 us (3%)
  starting transfers between devices  4.78 us (1%)
    pallas_call x1, Pallas kernels, make_exit(): return call(*given, *grads, small, vec)  84.2 us
    pallas_call x1, Pallas kernels, enter(): return call(hid, cot, ids, qv, ub, wq, wo, *vecs)  73.5 us
    pallas_call x1, Pallas kernels, make_back(): return call(gi, wu, act, wd, grads_u, grads_d, mid, cot, *vecs)  59.9 us
    pallas_call x1, Pallas kernels, make_mid(): return call(att, wo, own, *vecs, wu, wd, pieces, cot_own, cot_near)  48.5 us
    pallas_call x1, Pallas kernels, attn_bwd(): pl.pallas_call(functools.partial(attn_bwd_kernel, heads, shard), out_shap...  24.6 us
    pallas_call x1, Pallas kernels, attn_fwd(): pl.pallas_call(functools.partial(attn_fwd_kernel, heads, shard), out_shap...  22.1 us
    dot_general x6, matrix products, mm_tn(): lax.dot_general(a, b, (((0,), (0,)), ((), ())), preferred_element_type=F32)  20.9 us
    dot_general x1, matrix products, mm_nt(): lax.dot_general(a, b, (((1,), (1,)), ((), ())), preferred_element_type=F32)  9.14 us
  transfers between devices with their start and end apart: 4, of which 2 were waited for; matrix products, arithmetic and copies ran while one was open for 2% of the time, Pallas kernels for 12%

profile of v2, /device:TPU:1, one launch (start us, length us, event | category | flops | bytes accessed | tf_op | source)
XLA Modules:
  0.0 393.8 jit_solution(9599630056713400697)
XLA Ops:
  0.6 0.0 slice-start
  0.7 0.0 slice-start.1
  0.7 1.4 constant_dynamic-slice_fusion
  2.7 0.7 fusion.8
  3.5 0.8 convert_reduce_fusion
  4.3 0.1 slice.48
  4.4 0.1 concatenate.15
  4.5 0.6 broadcast_in_dim.51.ids
  5.1 0.0 slice-done
  5.1 0.0 slice-done.1
  5.1 0.1 pad_maximum_fusion
  5.2 73.5 %enter.1 = (bf16[320,1120]{1,0:T(8,128)(2,1)}, bf16[1280,1120]{1,0:T(8,128)(2,1)}, bf16[320,1120]{1,0:T(8,128)(2,1)}, s32[1,1408]{1,0:T(1,128)}, f32[2,280]{1,0:...) custom-call(bf16[320,1120]{1,0:T(8,128)(2,1)} %bitcast.38, ...), custom_call_target="tpu_custom_call" | custom-call | tf_op jit(solution)/shard_map/enter/pallas_call | solution.py:1094
  78.7 1.3 collective-permute-start
  80.0 0.1 collective-permute-start.1
  80.1 0.7 slice_bitcast_fusion.1
  80.8 0.6 pad_add_fusion.meta
  81.4 22.1 %attn_fwd.1 = (bf16[1280,280]{1,0:T(8,128)(2,1)}, f32[8,1280]{1,0:T(8,128)}, bf16[1280,384]{1,0:T(8,128)(2,1)}, bf16[1280,384]{1,0:T(8,128)(2,1)}, bf16[1280,384]{1,0:T(8,128)(2,1)}) custom-call(s32[6]{0:T(128)} %pad_add_fusion.meta, s32[1,1408]{1,0:T(1,128)} %get-tuple-element.55.start, bf16[1280,1120]{1,0:T(8,128)(2,1)} %get-tuple-element.58.normed, ...), custom_call_target="tpu_custom_call" | custom-call | flops 1376256000 | bytes 5734400 | tf_op jit(solution)/shard_map/attn_fwd/pallas_call | solution.py:236
  103.5 8.4 %collective-permute-done.1.cot_near = bf16[320,1120]{1,0:T(8,128)(2,1)} collective-permute-done((bf16[320,1120]{1,0:T(8,128)(2,1)}, bf16[320,1120]{1,0:T(8,128)(2,1)}, u32[]{:S(2)}, u32[]{:S(2)}) %collective-permute-start.1) | collective-permute-done | bytes 716832 | tf_op jit(solution)/shard_map/ppermute | solution.py:1215
  111.9 0.0 collective-permute-done.pieces
  111.9 1.1 copy-done.8
  113.0 48.5 %mid.1 = (f32[320,1120]{1,0:T(8,128)}, bf16[1280,1120]{1,0:T(8,128)(2,1)}, bf16[1280,1120]{1,0:T(8,128)(2,1)}, bf16[1120,1120]{1,0:T(8,128)(2,1)}, bf16[1120,1120]{1,0:T(8,128)(2,1)}) custom-call(bf16[1280,280]{1,0:T(8,128)(2,1)} %get-tuple-element.61.att.o, bf16[280,1120]{1,0:T(8,128)(2,1)} %get-tuple-element.62.wo, ...), custom_call_target="tpu_custom_call" | custom-call | tf_op jit(solution)/shard_map/mid/pallas_call | solution.py:1106
  161.5 0.0 copy-done.16
  161.5 0.0 copy-start.2
  161.5 7.7 %multiply_convert_fusion = (bf16[1280,1120]{1,0:T(8,128)(2,1)S(1)}, f32[1280,1120]{1,0:T(8,128)S(1)}) fusion(f32[1120]{0:T(1024)S(1)} %copy-done.16, bf16[1280,1120]{1,0:T(8,128)(2,1)} %get-tuple-element.68, bf16[1120,1120]{1,0:T(8,128)(2,1)} %get-tuple-element.69.wu), kind=kOutput, calls=%fused_computation.14 | convolution fusion | flops 3225600000 | bytes 13982080 | tf_op jit(solution)/shard_map/dot_general | solution.py:20
  169.2 0.0 copy-start.3
  169.2 0.0 copy-done.2
  169.2 0.0 copy-start.5
  169.2 5.5 %convolution_convert_fusion.raw_d = bf16[1120,1120]{1,0:T(8,128)(2,1)} fusion(bf16[1280,1120]{1,0:T(8,128)(2,1)S(1)} %get-tuple-element.107.act, bf16[1280,1120]{1,0:T(8,128)(2,1)S(1)} %copy-done.2), kind=kOutput, calls=%fused_computation.4 | convolution fusion | flops 3212518400 | bytes 8243200 | tf_op jit(solution)/shard_map/dot_general | solution.py:28
  174.7 0.0 copy-done.3
  174.7 0.0 copy-done.5
  174.7 9.1 %convert_reduce_fusion.1 = (f32[1120]{0:T(1024)S(1)}, bf16[1280,1120]{1,0:T(8,128)(2,1)S(1)}) fusion(f32[1280,1120]{1,0:T(8,128)S(1)} %get-tuple-element.108, bf16[1280,1120]{1,0:T(8,128)(2,1)S(1)} %copy-done.2, bf16[1120,1120]{1,0:T(8,128)(2,1)S(1)} %copy-done.5), kind=kOutput, calls=%fused_computation.13 | convolution fusion | flops 3241368576 | bytes 13982080 | tf_op jit(solution)/shard_map/dot_general | solution.py:24
  183.8 0.0 copy-start.4
  183.9 5.5 %convolution_convert_fusion.1.raw_u = bf16[1120,1120]{1,0:T(8,128)(2,1)} fusion(bf16[1280,1120]{1,0:T(8,128)(2,1)S(1)} %copy-done.15, bf16[1280,1120]{1,0:T(8,128)(2,1)S(1)} %get-tuple-element.110.gi), kind=kOutput, calls=%fused_computation.5 | convolution fusion | flops 3212518400 | bytes 8243200 | tf_op jit(solution)/shard_map/dot_general | solution.py:28
  189.4 59.9 %back.1 = (f32[320,1120]{1,0:T(8,128)}, bf16[1280,1120]{1,0:T(8,128)(2,1)}, f32[320,1120]{1,0:T(8,128)}, bf16[320,1120]{1,0:T(8,128)(2,1)}, bf16[576,1120]{1,0:T(8,128)(2,1)}, /*index=5*/f32[8,1120]{1,0:T(8,128)}) custom-call(bf16[1280,1120]{1,0:T(8,128)(2,1)} %copy-done.4, bf16[1120,1120]{1,0:T(8,128)(2,1)} %get-tuple-element.69.wu, ...), custom_call_target="tpu_custom_call" | custom-call | tf_op jit(solution)/shard_map/back/pallas_call | solution.py:1132
  249.2 3.3 collective-permute-start.3
  252.5 0.2 collective-permute-start.2
  252.6 0.8 slice.52
  253.4 24.6 %attn_bwd.1 = (bf16[1280,280]{1,0:T(8,128)(2,1)}, bf16[1280,280]{1,0:T(8,128)(2,1)}, bf16[1280,280]{1,0:T(8,128)(2,1)}) custom-call(s32[6]{0:T(128)} %pad_add_fusion.meta, s32[1,1408]{1,0:T(1,128)} %get-tuple-element.55.start, bf16[1280,384]{1,0:T(8,128)(2,1)} %get-tuple-element.74.qs, bf16[1280,384]{1,0:T(8,128)(2,1)} %get-tuple-element.75.ks, ...), custom_call_target="tpu_custom_call" | custom-call | flops 3670016000 | bytes 5734400 | tf_op jit(solution)/shard_map/attn_bwd/pallas_call | solution.py:265
  278.0 0.0 copy-done.11
  278.1 4.0 %convolution_convert_fusion.2.refs_13_ = bf16[280,1120]{1,0:T(8,128)(2,1)} fusion(bf16[1280,280]{1,0:T(8,128)(2,1)S(1)} %copy-done.11, bf16[1280,1120]{1,0:T(8,128)(2,1)} %get-tuple-element.77.gm), kind=kOutput, calls=%fused_computation.16 | convolution fusion | flops 803129600 | bytes 4211200 | tf_op jit(solution)/shard_map/dot_general | solution.py:28
  282.1 3.1 collective-permute-done.2.refs_1_
  285.2 0.2 convert_reduce_fusion.3
  285.4 2.0 convolution_convert_fusion.5.refs_10_
  287.4 0.0 collective-permute-done.3.refs_7_
  287.4 0.0 copy-done.1
  287.4 0.2 convert_reduce_fusion.2
  287.6 2.0 convolution_convert_fusion.3.refs_12_
  289.6 0.0 copy-done.9
  289.6 2.0 convolution_convert_fusion.4.refs_11_
  291.6 0.1 select_maximum_fusion
  291.6 0.1 broadcast_select_fusion
  291.7 1.3 concatenate.19.refs_14_
  293.0 84.2 %exit.1 = (bf16[320,1120]{1,0:T(8,128)(2,1)}, bf16[320,1120]{1,0:T(8,128)(2,1)}, bf16[1152,1120]{1,0:T(8,128)(2,1)}, bf16[1152,1120]{1,0:T(8,128)(2,1)}, bf16[1152,1120]{1,0:T(8,128)(2,1)}, /*index=5*/f32[16,1120]{1,0:T(8,128)}) custom-call(f32[320,1120]{1,0:T(8,128)} %get-tuple-element.72.refs_0_, bf16[320,1120]{1,0:T(8,128)(2,1)} %collective-permute-done.2.refs_1_, ...), custom_call_target="tpu_custom_call" | custom-call | tf_op jit(solution)/shard_map/exit/pallas_call | solution.py:1167
  377.2 0.0 copy-start.7
  377.2 3.8 convert_bitcast_fusion
  381.0 2.2 fusion.6
  383.2 2.7 slice_convert_fusion
  385.9 0.2 copy-done.6
  386.1 2.7 slice_convert_fusion.1
  388.8 1.7 slice_reduce_fusion
  390.5 0.7 dynamic-slice_reduce_fusion.1
  391.2 0.7 reshape_squeeze.3
  391.9 0.9 copy.39
  392.8 0.9 copy.40
  (25 shorter events, 0.1 us)
Async XLA Ops:
  0.6 4.4 %slice-start = ((bf16[1120,1120]{1,0:T(8,128)(2,1)}), bf16[32,1120]{1,0:T(8,128)(2,1)S(1)}, s32[]{:S(2)}) async-start(bf16[1120,1120]{1,0:T(8,128)(2,1)} %wu.1), calls=%async_computation | async-start | bytes 147456 | tf_op jit(solution)/shard_map/slice | solution.py:1213
  0.7 4.4 %slice-start.1 = ((bf16[1120,1120]{1,0:T(8,128)(2,1)}), bf16[32,1120]{1,0:T(8,128)(2,1)S(1)}, s32[]{:S(2)}) async-start(bf16[1120,1120]{1,0:T(8,128)(2,1)} %wd.1), calls=%async_computation.1 | async-start | bytes 147456 | tf_op jit(solution)/shard_map/slice | solution.py:1213
  78.7 33.2 %collective-permute-start = (bf16[608,1120]{1,0:T(8,128)(2,1)S(1)}, bf16[608,1120]{1,0:T(8,128)(2,1)S(1)}, u32[]{:S(2)}, u32[]{:S(2)}) collective-permute-start(bf16[608,1120]{1,0:T(8,128)(2,1)S(1)} %pad_maximum_fusion), channel_id=1, source_target_pairs={{0,2},{1,3},{6,4},{7,5},{8,10},{9,11},{14,12},{15,13},{16,18},{17,... | collective-permute-start | bytes 4085768 | tf_op jit(solution)/shard_map/ppermute | solution.py:1216
  80.0 31.9 %collective-permute-start.1 = (bf16[320,1120]{1,0:T(8,128)(2,1)}, bf16[320,1120]{1,0:T(8,128)(2,1)}, u32[]{:S(2)}, u32[]{:S(2)}) collective-permute-start(bf16[320,1120]{1,0:T(8,128)(2,1)} %get-tuple-element.65.cot_own), channel_id=1, source_target_pairs={{0,1},{1,0},{2,3},{3,2},{4,5},{5,4},{6,7},{7,6},{8,9},{9,8},{10,11... | collective-permute-start | bytes 2150408 | tf_op jit(solution)/shard_map/ppermute | solution.py:1215
  111.9 1.1 copy-start.8
  113.0 48.5 %copy-start.16 = (f32[1120]{0:T(1024)S(1)}, f32[1120]{0:T(1024)}, u32[]{:S(2)}) copy-start(f32[1120]{0:T(1024)} %get-tuple-element.70) | copy-start | bytes 13444
  161.5 7.7 %copy-start.2 = (bf16[1280,1120]{1,0:T(8,128)(2,1)S(1)}, bf16[1280,1120]{1,0:T(8,128)(2,1)}, u32[]{:S(2)}) copy-start(bf16[1280,1120]{1,0:T(8,128)(2,1)} %get-tuple-element.66.cot_full) | copy-start | bytes 8601604
  169.2 5.5 %copy-start.3 = (bf16[1280,1120]{1,0:T(8,128)(2,1)}, bf16[1280,1120]{1,0:T(8,128)(2,1)S(1)}, u32[]{:S(2)}) copy-start(bf16[1280,1120]{1,0:T(8,128)(2,1)S(1)} %get-tuple-element.107.act) | copy-start | bytes 8601604
  169.2 5.5 %copy-start.5 = (bf16[1120,1120]{1,0:T(8,128)(2,1)S(1)}, bf16[1120,1120]{1,0:T(8,128)(2,1)}, u32[]{:S(2)}) copy-start(bf16[1120,1120]{1,0:T(8,128)(2,1)} %get-tuple-element.67.wd) | copy-start | bytes 7526404
  174.7 9.2 %copy-start.15 = (bf16[1280,1120]{1,0:T(8,128)(2,1)S(1)}, bf16[1280,1120]{1,0:T(8,128)(2,1)}, u32[]{:S(2)}) copy-start(bf16[1280,1120]{1,0:T(8,128)(2,1)} %get-tuple-element.68) | copy-start | bytes 8601604
  183.8 5.5 %copy-start.4 = (bf16[1280,1120]{1,0:T(8,128)(2,1)}, bf16[1280,1120]{1,0:T(8,128)(2,1)S(1)}, u32[]{:S(2)}) copy-start(bf16[1280,1120]{1,0:T(8,128)(2,1)S(1)} %get-tuple-element.110.gi) | copy-start | bytes 8601604
  249.2 38.2 %collective-permute-start.3 = (bf16[576,1120]{1,0:T(8,128)(2,1)}, bf16[576,1120]{1,0:T(8,128)(2,1)S(1)}, u32[]{:S(2)}, u32[]{:S(2)}) collective-permute-start(bf16[576,1120]{1,0:T(8,128)(2,1)} %get-tuple-element.82.refs_6_), channel_id=1, source_target_pairs={{2,0},{3,1},{4,6},{5,7},{10,8},{11,9},{12,14},{13,15},{18,16},{19,... | collective-permute-start | bytes 3870728 | tf_op jit(solution)/shard_map/ppermute | solution.py:1258
  252.5 32.7 %collective-permute-start.2 = (bf16[320,1120]{1,0:T(8,128)(2,1)}, bf16[320,1120]{1,0:T(8,128)(2,1)}, u32[]{:S(2)}, u32[]{:S(2)}) collective-permute-start(bf16[320,1120]{1,0:T(8,128)(2,1)} %get-tuple-element.73), channel_id=1, source_target_pairs={{0,1},{1,0},{2,3},{3,2},{4,5},{5,4},{6,7},{7,6},{8,9},{9,8},{10,11... | collective-permute-start | bytes 2150408 | tf_op jit(solution)/shard_map/ppermute | solution.py:1259
  253.4 24.6 %copy-start.11 = (bf16[1280,280]{1,0:T(8,128)(2,1)S(1)}, bf16[1280,280]{1,0:T(8,128)(2,1)}, u32[]{:S(2)}) copy-start(bf16[1280,280]{1,0:T(8,128)(2,1)} %get-tuple-element.61.att.o) | copy-start | bytes 2150404
  278.0 7.1 %copy-start = (bf16[1280,280]{1,0:T(8,128)(2,1)S(1)}, bf16[1280,280]{1,0:T(8,128)(2,1)}, u32[]{:S(2)}) copy-start(bf16[1280,280]{1,0:T(8,128)(2,1)} %get-tuple-element.81.refs_2_) | copy-start | bytes 2150404
  278.1 7.3 %copy-start.14 = (bf16[1280,1120]{1,0:T(8,128)(2,1)S(1)}, bf16[1280,1120]{1,0:T(8,128)(2,1)}, u32[]{:S(2)}) copy-start(bf16[1280,1120]{1,0:T(8,128)(2,1)} %get-tuple-element.58.normed) | copy-start | bytes 8601604
  285.4 2.0 copy-start.1
  287.4 2.2 copy-start.9
  287.6 2.0 copy-start.10
  377.2 6.1 %copy-start.7 = (bf16[1152,1120]{1,0:T(8,128)(2,1)S(1)}, bf16[1152,1120]{1,0:T(8,128)(2,1)}, u32[]{:S(2)}) copy-start(bf16[1152,1120]{1,0:T(8,128)(2,1)} %get-tuple-element.95) | copy-start | bytes 7741444
  383.2 2.9 copy-start.6
  386.1 5.8 %copy-start.13 = (bf16[320,1120]{1,0:T(8,128)(2,1)S(1)}, bf16[320,1120]{1,0:T(8,128)(2,1)}, u32[]{:S(2)}) copy-start(bf16[320,1120]{1,0:T(8,128)(2,1)} %get-tuple-element.90) | copy-start | bytes 2150404
  386.1 6.7 %copy-start.12 = (bf16[320,1120]{1,0:T(8,128)(2,1)S(1)}, bf16[320,1120]{1,0:T(8,128)(2,1)}, u32[]{:S(2)}) copy-start(bf16[320,1120]{1,0:T(8,128)(2,1)} %get-tuple-element.91) | copy-start | bytes 2150404

commit v3 on v2

--- a/solution.py
+++ b/solution.py
@@ -677,7 +677,8 @@
 
 def enter_kernel(
     columns, shard, hid, cot, ids, qv, ub, wq, wo, gain, shift,
-    own, full, cot_own, ids_o, qv_o, ub_o, wq_o, wo_o, send_sems, recv_sems, local_sems,
+    own_out, full_out, cot_out, ids_o, qv_o, ub_o, wq_out, wo_out,
+    own, full, cot_own, wq_o, wo_o, send_sems, recv_sems, local_sems,
 ):
     place, link = Place(columns), Link(send_sems, recv_sems)
     n = shard // CHUNKS
@@ -720,13 +721,20 @@
         core.append(gather_relay(link, place, full, shard, i, near[i]))
     for weight in weights:
         weight.share()
+    stores = Local(local_sems, None, 8)
+    stores.keep(own, own_out)
     for copy in core:
         copy.wait_recv()
-    for weight in weights:
-        weight.drain()
+    stores.keep(full, full_out)
     for copy in (ids_copy, qv_copy, ub_copy, cot_copy):
         arrive(copy, away)
     local.drain(CHUNKS)
+    stores.keep(cot_own, cot_out)
+    for weight in weights:
+        weight.drain()
+    stores.keep(wq_o, wq_out)
+    stores.keep(wo_o, wo_out)
+    stores.drain()
     link.close()
 
 
@@ -812,12 +820,14 @@
 
 
 def back_kernel(
-    columns, shard, gi, wu, act, wd, raw_u, raw_d, mid, cot_full, gain, bias, *refs
+    columns, shard, *refs
 ):
     place, link = Place(columns), Link(*refs[-3:-1])
     bits = place.bits
-    gmid, full, res, res_near, slices, sums = refs[:6]
-    scratch = list(refs[6:-3])
+    given, (raw_u, raw_d, cot_full, gain, bias), refs = refs[:5], refs[5:10], refs[10:]
+    (res_o, near_o, gmid_o, full_o, slices_o), sums = refs[:5], refs[5]
+    held, (res, res_near, gmid, full, slices), scratch = refs[6:11], refs[11:16], list(refs[16:-3])
+    gi, wu, act, wd, mid = held
     a_bufs, b_bufs = scratch[:4], scratch[4:6]
     cot, grads_u, grads_d = scratch[6:9]
     halves = scratch[9:]
@@ -826,6 +836,10 @@
     pack(local, [raw_u], grads_u)
     pack(local, [raw_d], grads_d)
     local.keep(rows_of(cot_full, 0, shard), cot)
+    loads = Local(refs[-1], None, 3)
+    for src, dst in zip(given, held):
+        loads.keep(src, dst)
+    stores = Local(refs[-1], None, 8)
     meet([place.core, place.near] + [place.column(1 << b) for b in range(bits)])
 
     def make(rows):
@@ -848,10 +862,14 @@
     local.drain()
     half_u.start(0)
     half_d.start(0)
+    for copy in loads.copies[:2]:
+        copy.wait()
     total.start()
     for i in range(CHUNKS):
         total.pass_on(i)
     total.rest()
+    for copy in loads.copies[2:]:
+        copy.wait()
     total2.start()
     total2.rest()
     for copy in total2.core.values():
@@ -889,6 +907,9 @@
     if bits > 1:
         half_u.start(1)
         half_d.start(1)
+    stores.keep(res, res_o)
+    stores.keep(res_near, near_o)
+    stores.keep(gmid, gmid_o)
     for i in range(CHUNKS):
         core.append(gather_relay(link, place, full, shard, i, near[i]))
     for s in range(1, bits):
@@ -900,6 +921,9 @@
             half_d.start(s + 1)
     for copy in core:
         copy.wait_recv()
+    stores.keep(full, full_o)
+    stores.keep(slices, slices_o)
+    stores.drain()
     link.close()
 
 
@@ -1089,7 +1113,8 @@
     shard, model = hid.shape
     outs = (like(hid), shaped((4 * shard, model), BF), like(cot), like(ids), like(qv), like(ub), like(wq), like(wo))
     call = remote_call(
-        "enter", functools.partial(enter_kernel, columns, shard), 0, outs, [any_space()] * 7 + [vmem()] * 2, []
+        "enter", functools.partial(enter_kernel, columns, shard), 0, outs, [any_space()] * 7 + [vmem()] * 2,
+        held_like([outs[j] for j in (0, 1, 2, 6, 7)]), away=(0, 1, 2, 6, 7),
     )
     return call(hid, cot, ids, qv, ub, wq, wo, *vecs)
 
@@ -1109,11 +1134,12 @@
 def make_back(columns, size, gi, wu, act, wd, grads_u, grads_d, mid, cot, *vecs):
     shard, model = mid.shape
     bits = columns.bit_length() - 1
+    given = (gi, wu, act, wd, mid)
     outs = (
         shaped((shard, model), F32),
+        shaped((shard, model), BF),
+        shaped((shard, model), F32),
         shaped((4 * shard, model), BF),
-        shaped((shard, model), F32),
-        shaped((shard, model), BF),
         shaped((2 * (size // columns), model), BF),
         shaped((8, model), F32),
     )
@@ -1121,15 +1147,18 @@
     halves = per_side[: bits - 1] + per_side
     call = remote_call(
         "back", functools.partial(back_kernel, columns, shard), 2, outs,
-        [vmem()] * 4 + [any_space()] * 2 + [vmem(), any_space(), vmem(), vmem()],
-        scatter_scratch(shard, model)
+        [any_space()] * 8 + [vmem()] * 2,
+        held_like(given)
+        + held_like(outs[:5])
+        + scatter_scratch(shard, model)
         + scatter_scratch(shard, model)[:2]
         + [pltpu.VMEM((shard, model), BF)]
         + [pltpu.VMEM((size, model), BF)] * 2
         + halves
         + halves,
-    )
-    return call(gi, wu, act, wd, grads_u, grads_d, mid, cot, *vecs)
+        away=range(5),
+    )
+    return call(*given, grads_u, grads_d, cot, *vecs)
 
 
 def make_exit(columns, size, dq, dk, dv, wq, own, gmid, slices, far, res, res_near, grads, small, vec):
@@ -1241,7 +1270,7 @@
     grad_inner = (mm_nt(cot_full, w_down) * slope).astype(BF)
     unit = 32 * columns
     size = -(-model // unit) * unit
-    grad_mid, gm_full, res, res_near, slices, sums = make_back(
+    res, res_near, grad_mid, gm_full, slices, sums = make_back(
         columns,
         size,
         grad_inner,

time: 400 us -> 394 us (0.985)
    pallas_call x1, Pallas kernels: 59.9 us -> 55.4 us  [make_back(): return call(*given, grads_u, grads_d, cot, *vecs)]
  transfers between devices with their start and end apart: 4 -> 4, of which waited for: 2 -> 2; matrix products, arithmetic and copies ran while one was open for 2% -> 2% of each run, Pallas kernels for 12% -> 13%
where the time goes in v3:
time: 394 us; the launch traced here: 389 us
  Pallas kernels  310 us (79%)
  matrix products  37.7 us (10%)
  other arithmetic  14.2 us (4%)
  local copies, waits for them, and re-layouts  11.1 us (3%)
  waiting for transfers between devices  8.82 us (2%)
  starting transfers between devices  4.82 us (1%)
    pallas_call x1, Pallas kernels, make_exit(): return call(*given, *grads, small, vec)  84.2 us
    pallas_call x1, Pallas kernels, enter(): return call(hid, cot, ids, qv, ub, wq, wo, *vecs)  72.8 us
    pallas_call x1, Pallas kernels, make_back(): return call(*given, grads_u, grads_d, cot, *vecs)  55.4 us
    pallas_call x1, Pallas kernels, make_mid(): return call(att, wo, own, *vecs, wu, wd, pieces, cot_own, cot_near)  48.4 us
    pallas_call x1, Pallas kernels, attn_bwd(): pl.pallas_call(functools.partial(attn_bwd_kernel, heads, shard), out_shap...  26.1 us
    pallas_call x1, Pallas kernels, attn_fwd(): pl.pallas_call(functools.partial(attn_fwd_kernel, heads, shard), out_shap...  23.3 us
    dot_general x6, matrix products, mm_tn(): lax.dot_general(a, b, (((0,), (0,)), ((), ())), preferred_element_type=F32)  20.9 us
    dot_general x1, matrix products, mm_nt(): lax.dot_general(a, b, (((1,), (1,)), ((), ())), preferred_element_type=F32)  9.14 us
  transfers between devices with their start and end apart: 4, of which 2 were waited for; matrix products, arithmetic and copies ran while one was open for 2% of the time, Pallas kernels for 13%

profile of v3, /device:TPU:1, one launch (start us, length us, event | category | flops | bytes accessed | tf_op | source)
XLA Modules:
  0.0 388.6 jit_solution(15928606259435892078)
XLA Ops:
  0.6 0.0 slice-start
  0.7 0.0 slice-start.1
  0.7 1.4 constant_dynamic-slice_fusion
  2.7 0.7 fusion.8
  3.5 0.8 convert_reduce_fusion
  4.3 0.1 slice.48
  4.4 0.1 concatenate.15
  4.5 0.6 broadcast_in_dim.51.ids
  5.1 0.0 slice-done
  5.1 0.1 pad_maximum_fusion
  5.2 72.8 %enter.1 = (bf16[320,1120]{1,0:T(8,128)(2,1)}, bf16[1280,1120]{1,0:T(8,128)(2,1)}, bf16[320,1120]{1,0:T(8,128)(2,1)}, s32[1,1408]{1,0:T(1,128)}, f32[2,280]{1,0:...) custom-call(bf16[320,1120]{1,0:T(8,128)(2,1)} %bitcast.38, ...), custom_call_target="tpu_custom_call" | custom-call | tf_op jit(solution)/shard_map/enter/pallas_call | solution.py:1119
  78.0 1.3 collective-permute-start
  79.3 0.1 collective-permute-start.1
  79.3 0.7 slice_bitcast_fusion.1
  80.0 0.6 pad_add_fusion.meta
  80.6 23.3 %attn_fwd.1 = (bf16[1280,280]{1,0:T(8,128)(2,1)}, f32[8,1280]{1,0:T(8,128)}, bf16[1280,384]{1,0:T(8,128)(2,1)}, bf16[1280,384]{1,0:T(8,128)(2,1)}, bf16[1280,384]{1,0:T(8,128)(2,1)}) custom-call(s32[6]{0:T(128)} %pad_add_fusion.meta, s32[1,1408]{1,0:T(1,128)} %get-tuple-element.55.start, bf16[1280,1120]{1,0:T(8,128)(2,1)} %get-tuple-element.58.normed, ...), custom_call_target="tpu_custom_call" | custom-call | flops 1376256000 | bytes 5734400 | tf_op jit(solution)/shard_map/attn_fwd/pallas_call | solution.py:236
  103.9 7.2 %collective-permute-done.1.cot_near = bf16[320,1120]{1,0:T(8,128)(2,1)} collective-permute-done((bf16[320,1120]{1,0:T(8,128)(2,1)}, bf16[320,1120]{1,0:T(8,128)(2,1)}, u32[]{:S(2)}, u32[]{:S(2)}) %collective-permute-start.1) | collective-permute-done | bytes 716832 | tf_op jit(solution)/shard_map/ppermute | solution.py:1244
  111.1 0.0 collective-permute-done.pieces
  111.1 1.1 copy-done.8
  112.2 48.4 %mid.1 = (f32[320,1120]{1,0:T(8,128)}, bf16[1280,1120]{1,0:T(8,128)(2,1)}, bf16[1280,1120]{1,0:T(8,128)(2,1)}, bf16[1120,1120]{1,0:T(8,128)(2,1)}, bf16[1120,1120]{1,0:T(8,128)(2,1)}) custom-call(bf16[1280,280]{1,0:T(8,128)(2,1)} %get-tuple-element.61.att.o, bf16[280,1120]{1,0:T(8,128)(2,1)} %get-tuple-element.62.wo, ...), custom_call_target="tpu_custom_call" | custom-call | tf_op jit(solution)/shard_map/mid/pallas_call | solution.py:1131
  160.7 0.0 copy-done.16
  160.7 0.0 copy-start.2
  160.7 7.7 %multiply_convert_fusion = (bf16[1280,1120]{1,0:T(8,128)(2,1)S(1)}, f32[1280,1120]{1,0:T(8,128)S(1)}) fusion(f32[1120]{0:T(1024)S(1)} %copy-done.16, bf16[1280,1120]{1,0:T(8,128)(2,1)} %get-tuple-element.68, bf16[1120,1120]{1,0:T(8,128)(2,1)} %get-tuple-element.69.refs_1_), kind=kOutput, calls=%fused_computation.14 | convolution fusion | flops 3225600000 | bytes 13982080 | tf_op jit(solution)/shard_map/dot_general | solution.py:20
  168.4 0.0 copy-start.3
  168.4 0.0 copy-done.2
  168.4 0.0 copy-start.5
  168.4 5.5 %convolution_convert_fusion.refs_6_ = bf16[1120,1120]{1,0:T(8,128)(2,1)} fusion(bf16[1280,1120]{1,0:T(8,128)(2,1)S(1)} %get-tuple-element.107.refs_2_, bf16[1280,1120]{1,0:T(8,128)(2,1)S(1)} %copy-done.2), kind=kOutput, calls=%fused_computation.4 | convolution fusion | flops 3212518400 | bytes 8243200 | tf_op jit(solution)/shard_map/dot_general | solution.py:28
  173.9 0.0 copy-done.3
  173.9 9.1 %convert_reduce_fusion.1 = (f32[1120]{0:T(1024)S(1)}, bf16[1280,1120]{1,0:T(8,128)(2,1)S(1)}) fusion(f32[1280,1120]{1,0:T(8,128)S(1)} %get-tuple-element.108, bf16[1280,1120]{1,0:T(8,128)(2,1)S(1)} %copy-done.2, bf16[1120,1120]{1,0:T(8,128)(2,1)S(1)} %copy-done.5), kind=kOutput, calls=%fused_computation.13 | convolution fusion | flops 3241368576 | bytes 13982080 | tf_op jit(solution)/shard_map/dot_general | solution.py:24
  183.0 0.0 copy-start.4
  183.0 0.0 copy-done.15
  183.0 5.5 %convolution_convert_fusion.1.refs_5_ = bf16[1120,1120]{1,0:T(8,128)(2,1)} fusion(bf16[1280,1120]{1,0:T(8,128)(2,1)S(1)} %copy-done.15, bf16[1280,1120]{1,0:T(8,128)(2,1)S(1)} %get-tuple-element.110.refs_0_), kind=kOutput, calls=%fused_computation.5 | convolution fusion | flops 3212518400 | bytes 8243200 | tf_op jit(solution)/shard_map/dot_general | solution.py:28
  188.6 55.4 %back.1 = (f32[320,1120]{1,0:T(8,128)}, bf16[320,1120]{1,0:T(8,128)(2,1)}, f32[320,1120]{1,0:T(8,128)}, bf16[1280,1120]{1,0:T(8,128)(2,1)}, bf16[576,1120]{1,0:T(8,128)(2,1)}, /*index=5*/f32[8,1120]{1,0:T(8,128)}) custom-call(bf16[1280,1120]{1,0:T(8,128)(2,1)} %copy-done.4, bf16[1120,1120]{1,0:T(8,128)(2,1)} %get-tuple-element.69.refs_1_, ...), custom_call_target="tpu_custom_call" | custom-call | tf_op jit(solution)/shard_map/back/pallas_call | solution.py:1161
  244.0 3.3 collective-permute-start.3
  247.3 0.2 collective-permute-start.2
  247.5 0.8 slice.52
  248.2 26.1 %attn_bwd.1 = (bf16[1280,280]{1,0:T(8,128)(2,1)}, bf16[1280,280]{1,0:T(8,128)(2,1)}, bf16[1280,280]{1,0:T(8,128)(2,1)}) custom-call(s32[6]{0:T(128)} %pad_add_fusion.meta, s32[1,1408]{1,0:T(1,128)} %get-tuple-element.55.start, bf16[1280,384]{1,0:T(8,128)(2,1)} %get-tuple-element.74.qs, bf16[1280,384]{1,0:T(8,128)(2,1)} %get-tuple-element.75.ks, ...), custom_call_target="tpu_custom_call" | custom-call | flops 3670016000 | bytes 5734400 | tf_op jit(solution)/shard_map/attn_bwd/pallas_call | solution.py:265
  274.4 0.0 copy-start.14
  274.4 4.0 %convolution_convert_fusion.2.refs_13_ = bf16[280,1120]{1,0:T(8,128)(2,1)} fusion(bf16[1280,280]{1,0:T(8,128)(2,1)S(1)} %copy-done.11, bf16[1280,1120]{1,0:T(8,128)(2,1)} %get-tuple-element.77.gm), kind=kOutput, calls=%fused_computation.16 | convolution fusion | flops 803129600 | bytes 4211200 | tf_op jit(solution)/shard_map/dot_general | solution.py:28
  278.4 1.6 collective-permute-done.2.refs_1_
  280.0 0.0 copy-done
  280.0 0.2 convert_reduce_fusion.3
  280.2 2.0 convolution_convert_fusion.5.refs_10_
  282.2 0.0 collective-permute-done.3.refs_7_
  282.2 0.2 convert_reduce_fusion.2
  282.4 2.0 convolution_convert_fusion.3.refs_12_
  284.4 0.0 copy-done.10
  284.4 2.0 convolution_convert_fusion.4.refs_11_
  286.4 0.1 select_maximum_fusion
  286.4 0.1 broadcast_select_fusion
  286.5 1.3 concatenate.19.refs_14_
  287.8 84.2 %exit.1 = (bf16[320,1120]{1,0:T(8,128)(2,1)}, bf16[320,1120]{1,0:T(8,128)(2,1)}, bf16[1152,1120]{1,0:T(8,128)(2,1)}, bf16[1152,1120]{1,0:T(8,128)(2,1)}, bf16[1152,1120]{1,0:T(8,128)(2,1)}, /*index=5*/f32[16,1120]{1,0:T(8,128)}) custom-call(f32[320,1120]{1,0:T(8,128)} %get-tuple-element.72.refs_0_, bf16[320,1120]{1,0:T(8,128)(2,1)} %collective-permute-done.2.refs_1_, ...), custom_call_target="tpu_custom_call" | custom-call | tf_op jit(solution)/shard_map/exit/pallas_call | solution.py:1196
  372.0 3.8 convert_bitcast_fusion
  375.8 2.2 fusion.6
  378.0 0.0 copy-done.7
  378.1 2.7 slice_convert_fusion
  380.7 0.2 copy-done.6
  380.9 2.7 slice_convert_fusion.1
  383.6 1.7 slice_reduce_fusion
  385.3 0.7 dynamic-slice_reduce_fusion.1
  386.1 0.7 reshape_squeeze.3
  386.7 0.9 copy.39
  387.6 0.0 copy-done.12
  387.6 0.9 copy.40
  (25 shorter events, 0.1 us)
Async XLA Ops:
  0.6 4.4 %slice-start = ((bf16[1120,1120]{1,0:T(8,128)(2,1)}), bf16[32,1120]{1,0:T(8,128)(2,1)S(1)}, s32[]{:S(2)}) async-start(bf16[1120,1120]{1,0:T(8,128)(2,1)} %wu.1), calls=%async_computation | async-start | bytes 147456 | tf_op jit(solution)/shard_map/slice | solution.py:1242
  0.7 4.4 %slice-start.1 = ((bf16[1120,1120]{1,0:T(8,128)(2,1)}), bf16[32,1120]{1,0:T(8,128)(2,1)S(1)}, s32[]{:S(2)}) async-start(bf16[1120,1120]{1,0:T(8,128)(2,1)} %wd.1), calls=%async_computation.1 | async-start | bytes 147456 | tf_op jit(solution)/shard_map/slice | solution.py:1242
  78.0 33.2 %collective-permute-start = (bf16[608,1120]{1,0:T(8,128)(2,1)S(1)}, bf16[608,1120]{1,0:T(8,128)(2,1)S(1)}, u32[]{:S(2)}, u32[]{:S(2)}) collective-permute-start(bf16[608,1120]{1,0:T(8,128)(2,1)S(1)} %pad_maximum_fusion), channel_id=1, source_target_pairs={{0,2},{1,3},{6,4},{7,5},{8,10},{9,11},{14,12},{15,13},{16,18},{17,... | collective-permute-start | bytes 4085768 | tf_op jit(solution)/shard_map/ppermute | solution.py:1245
  79.3 31.9 %collective-permute-start.1 = (bf16[320,1120]{1,0:T(8,128)(2,1)}, bf16[320,1120]{1,0:T(8,128)(2,1)}, u32[]{:S(2)}, u32[]{:S(2)}) collective-permute-start(bf16[320,1120]{1,0:T(8,128)(2,1)} %get-tuple-element.65.cot_own), channel_id=1, source_target_pairs={{0,1},{1,0},{2,3},{3,2},{4,5},{5,4},{6,7},{7,6},{8,9},{9,8},{10,11... | collective-permute-start | bytes 2150408 | tf_op jit(solution)/shard_map/ppermute | solution.py:1244
  111.1 1.1 copy-start.8
  112.2 48.4 %copy-start.16 = (f32[1120]{0:T(1024)S(1)}, f32[1120]{0:T(1024)}, u32[]{:S(2)}) copy-start(f32[1120]{0:T(1024)} %get-tuple-element.70) | copy-start | bytes 13444
  160.7 7.7 %copy-start.2 = (bf16[1280,1120]{1,0:T(8,128)(2,1)S(1)}, bf16[1280,1120]{1,0:T(8,128)(2,1)}, u32[]{:S(2)}) copy-start(bf16[1280,1120]{1,0:T(8,128)(2,1)} %get-tuple-element.66.refs_7_) | copy-start | bytes 8601604
  168.4 5.5 %copy-start.3 = (bf16[1280,1120]{1,0:T(8,128)(2,1)}, bf16[1280,1120]{1,0:T(8,128)(2,1)S(1)}, u32[]{:S(2)}) copy-start(bf16[1280,1120]{1,0:T(8,128)(2,1)S(1)} %get-tuple-element.107.refs_2_) | copy-start | bytes 8601604
  168.4 5.5 %copy-start.5 = (bf16[1120,1120]{1,0:T(8,128)(2,1)S(1)}, bf16[1120,1120]{1,0:T(8,128)(2,1)}, u32[]{:S(2)}) copy-start(bf16[1120,1120]{1,0:T(8,128)(2,1)} %get-tuple-element.67.refs_3_) | copy-start | bytes 7526404
  173.9 9.2 %copy-start.15 = (bf16[1280,1120]{1,0:T(8,128)(2,1)S(1)}, bf16[1280,1120]{1,0:T(8,128)(2,1)}, u32[]{:S(2)}) copy-start(bf16[1280,1120]{1,0:T(8,128)(2,1)} %get-tuple-element.68) | copy-start | bytes 8601604
  183.0 5.5 %copy-start.4 = (bf16[1280,1120]{1,0:T(8,128)(2,1)}, bf16[1280,1120]{1,0:T(8,128)(2,1)S(1)}, u32[]{:S(2)}) copy-start(bf16[1280,1120]{1,0:T(8,128)(2,1)S(1)} %get-tuple-element.110.refs_0_) | copy-start | bytes 8601604
  244.0 38.2 %collective-permute-start.3 = (bf16[576,1120]{1,0:T(8,128)(2,1)}, bf16[576,1120]{1,0:T(8,128)(2,1)S(1)}, u32[]{:S(2)}, u32[]{:S(2)}) collective-permute-start(bf16[576,1120]{1,0:T(8,128)(2,1)} %get-tuple-element.82.refs_6_), channel_id=1, source_target_pairs={{2,0},{3,1},{4,6},{5,7},{10,8},{11,9},{12,14},{13,15},{18,16},{19,... | collective-permute-start | bytes 3870728 | tf_op jit(solution)/shard_map/ppermute | solution.py:1287
  247.3 32.7 %collective-permute-start.2 = (bf16[320,1120]{1,0:T(8,128)(2,1)}, bf16[320,1120]{1,0:T(8,128)(2,1)}, u32[]{:S(2)}, u32[]{:S(2)}) collective-permute-start(bf16[320,1120]{1,0:T(8,128)(2,1)} %get-tuple-element.73), channel_id=1, source_target_pairs={{0,1},{1,0},{2,3},{3,2},{4,5},{5,4},{6,7},{7,6},{8,9},{9,8},{10,11... | collective-permute-start | bytes 2150408 | tf_op jit(solution)/shard_map/ppermute | solution.py:1288
  248.2 26.1 %copy-start.11 = (bf16[1280,280]{1,0:T(8,128)(2,1)S(1)}, bf16[1280,280]{1,0:T(8,128)(2,1)}, u32[]{:S(2)}) copy-start(bf16[1280,280]{1,0:T(8,128)(2,1)} %get-tuple-element.61.att.o) | copy-start | bytes 2150404
  274.4 5.6 %copy-start = (bf16[1280,280]{1,0:T(8,128)(2,1)S(1)}, bf16[1280,280]{1,0:T(8,128)(2,1)}, u32[]{:S(2)}) copy-start(bf16[1280,280]{1,0:T(8,128)(2,1)} %get-tuple-element.81.refs_2_) | copy-start | bytes 2150404
  274.4 5.8 %copy-start.14 = (bf16[1280,1120]{1,0:T(8,128)(2,1)S(1)}, bf16[1280,1120]{1,0:T(8,128)(2,1)}, u32[]{:S(2)}) copy-start(bf16[1280,1120]{1,0:T(8,128)(2,1)} %get-tuple-element.58.normed) | copy-start | bytes 8601604
  280.2 2.0 copy-start.1
  282.2 2.2 copy-start.9
  282.4 2.0 copy-start.10
  372.0 6.1 %copy-start.7 = (bf16[1152,1120]{1,0:T(8,128)(2,1)S(1)}, bf16[1152,1120]{1,0:T(8,128)(2,1)}, u32[]{:S(2)}) copy-start(bf16[1152,1120]{1,0:T(8,128)(2,1)} %get-tuple-element.95) | copy-start | bytes 7741444
  378.1 2.9 copy-start.6
  380.9 5.8 %copy-start.13 = (bf16[320,1120]{1,0:T(8,128)(2,1)S(1)}, bf16[320,1120]{1,0:T(8,128)(2,1)}, u32[]{:S(2)}) copy-start(bf16[320,1120]{1,0:T(8,128)(2,1)} %get-tuple-element.90) | copy-start | bytes 2150404
  380.9 6.7 %copy-start.12 = (bf16[320,1120]{1,0:T(8,128)(2,1)S(1)}, bf16[320,1120]{1,0:T(8,128)(2,1)}, u32[]{:S(2)}) copy-start(bf16[320,1120]{1,0:T(8,128)(2,1)} %get-tuple-element.91) | copy-start | bytes 2150404

commit v4 on v3

--- a/solution.py
+++ b/solution.py
@@ -691,10 +691,6 @@
     swaps = [
         link.send(rows_of(hid, i * n, n), rows_of(own, i * n, n), place.swap, away) for i in range(CHUNKS)
     ]
-    for weight in weights:
-        weight.open()
-    qv_copy = link.send(qv, qv_o, place.far, home)
-    ub_copy = link.send(ub, ub_o, place.far, home)
     local = Local(local_sems, home)
     held = [local.keep(rows_of(hid, i * n, n), rows_of(own, i * n, n)) for i in range(CHUNKS)]
     local.keep(cot, cot_own)
@@ -716,6 +712,10 @@
         over_rows(i * n, n, STEP, rows)
         near[i], copy = gather_start(link, place, full, shard, i)
         core.append(copy)
+    for weight in weights:
+        weight.open()
+    qv_copy = link.send(qv, qv_o, place.far, home)
+    ub_copy = link.send(ub, ub_o, place.far, home)
     cot_copy = link.send(cot, cot_own, place.swap, away)
     for i in range(CHUNKS):
         core.append(gather_relay(link, place, full, shard, i, near[i]))

time: 394 us -> 390 us (0.990)
  Pallas kernels: 310 us -> 304 us
    ppermute x1, waiting for transfers between devices: 0.01 us -> 8.33 us  [body(): pieces = lax.ppermute(pieces, axes, to_away)]
    ppermute x1, waiting for transfers between devices: 7.23 us -> 1.09 us  [body(): cot_near = lax.ppermute(cot_own, axes, to_near)]
  transfers between devices with their start and end apart: 4 -> 4, of which waited for: 2 -> 3; matrix products, arithmetic and copies ran while one was open for 2% -> 2% of each run, Pallas kernels for 13% -> 12%
where the time goes in v4:
time: 390 us; the launch traced here: 384 us
  Pallas kernels  304 us (78%)
  matrix products  37.7 us (10%)
  other arithmetic  14.2 us (4%)
  local copies, waits for them, and re-layouts  11.1 us (3%)
  waiting for transfers between devices  10.2 us (3%)
  starting transfers between devices  4.78 us (1%)
    pallas_call x1, Pallas kernels, make_exit(): return call(*given, *grads, small, vec)  85.9 us
    pallas_call x1, Pallas kernels, enter(): return call(hid, cot, ids, qv, ub, wq, wo, *vecs)  69.1 us
    pallas_call x1, Pallas kernels, make_back(): return call(*given, grads_u, grads_d, cot, *vecs)  56.7 us
    pallas_call x1, Pallas kernels, make_mid(): return call(att, wo, own, *vecs, wu, wd, pieces, cot_own, cot_near)  45.7 us
    pallas_call x1, Pallas kernels, attn_bwd(): pl.pallas_call(functools.partial(attn_bwd_kernel, heads, shard), out_shap...  24.6 us
    pallas_call x1, Pallas kernels, attn_fwd(): pl.pallas_call(functools.partial(attn_fwd_kernel, heads, shard), out_shap...  22.1 us
    dot_general x6, matrix products, mm_tn(): lax.dot_general(a, b, (((0,), (0,)), ((), ())), preferred_element_type=F32)  20.9 us
    dot_general x1, matrix products, mm_nt(): lax.dot_general(a, b, (((1,), (1,)), ((), ())), preferred_element_type=F32)  9.14 us
  transfers between devices with their start and end apart: 4, of which 3 were waited for; matrix products, arithmetic and copies ran while one was open for 2% of the time, Pallas kernels for 12%

profile of v4, /device:TPU:1, one launch (start us, length us, event | category | flops | bytes accessed | tf_op | source)
XLA Modules:
  0.0 383.9 jit_solution(4758076894543354021)
XLA Ops:
  0.6 0.0 slice-start
  0.7 0.0 slice-start.1
  0.7 1.4 constant_dynamic-slice_fusion
  2.7 0.7 fusion.8
  3.5 0.8 convert_reduce_fusion
  4.3 0.1 slice.48
  4.4 0.1 concatenate.15
  4.5 0.6 broadcast_in_dim.51.ids
  5.1 0.0 slice-done
  5.1 0.0 slice-done.1
  5.1 0.1 pad_maximum_fusion
  5.2 69.1 %enter.1 = (bf16[320,1120]{1,0:T(8,128)(2,1)}, bf16[1280,1120]{1,0:T(8,128)(2,1)}, bf16[320,1120]{1,0:T(8,128)(2,1)}, s32[1,1408]{1,0:T(1,128)}, f32[2,280]{1,0:...) custom-call(bf16[320,1120]{1,0:T(8,128)(2,1)} %bitcast.38, ...), custom_call_target="tpu_custom_call" | custom-call | tf_op jit(solution)/shard_map/enter/pallas_call | solution.py:1119
  74.3 1.3 collective-permute-start
  75.6 0.1 collective-permute-start.1
  75.7 0.7 slice_bitcast_fusion.1
  76.4 0.6 pad_add_fusion.meta
  77.0 22.1 %attn_fwd.1 = (bf16[1280,280]{1,0:T(8,128)(2,1)}, f32[8,1280]{1,0:T(8,128)}, bf16[1280,384]{1,0:T(8,128)(2,1)}, bf16[1280,384]{1,0:T(8,128)(2,1)}, bf16[1280,384]{1,0:T(8,128)(2,1)}) custom-call(s32[6]{0:T(128)} %pad_add_fusion.meta, s32[1,1408]{1,0:T(1,128)} %get-tuple-element.55.start, bf16[1280,1120]{1,0:T(8,128)(2,1)} %get-tuple-element.58.normed, ...), custom_call_target="tpu_custom_call" | custom-call | flops 1376256000 | bytes 5734400 | tf_op jit(solution)/shard_map/attn_fwd/pallas_call | solution.py:236
  99.1 1.1 collective-permute-done.1.cot_near
  100.2 8.3 %collective-permute-done.pieces = bf16[608,1120]{1,0:T(8,128)(2,1)S(1)} collective-permute-done((bf16[608,1120]{1,0:T(8,128)(2,1)S(1)}, bf16[608,1120]{1,0:T(8,128)(2,1)S(1)}, u32[]{:S(2)}, u32[]{:S(2)}) %collective-permute-start) | collective-permute-done | bytes 1361952 | tf_op jit(solution)/shard_map/ppermute | solution.py:1245
  108.5 1.1 copy-done.8
  109.6 45.7 %mid.1 = (f32[320,1120]{1,0:T(8,128)}, bf16[1280,1120]{1,0:T(8,128)(2,1)}, bf16[1280,1120]{1,0:T(8,128)(2,1)}, bf16[1120,1120]{1,0:T(8,128)(2,1)}, bf16[1120,1120]{1,0:T(8,128)(2,1)}) custom-call(bf16[1280,280]{1,0:T(8,128)(2,1)} %get-tuple-element.61.att.o, bf16[280,1120]{1,0:T(8,128)(2,1)} %get-tuple-element.62.wo, ...), custom_call_target="tpu_custom_call" | custom-call | tf_op jit(solution)/shard_map/mid/pallas_call | solution.py:1131
  155.3 0.0 copy-done.16
  155.3 0.0 copy-start.2
  155.3 7.7 %multiply_convert_fusion = (bf16[1280,1120]{1,0:T(8,128)(2,1)S(1)}, f32[1280,1120]{1,0:T(8,128)S(1)}) fusion(f32[1120]{0:T(1024)S(1)} %copy-done.16, bf16[1280,1120]{1,0:T(8,128)(2,1)} %get-tuple-element.68, bf16[1120,1120]{1,0:T(8,128)(2,1)} %get-tuple-element.69.refs_1_), kind=kOutput, calls=%fused_computation.14 | convolution fusion | flops 3225600000 | bytes 13982080 | tf_op jit(solution)/shard_map/dot_general | solution.py:20
  163.0 0.0 copy-start.3
  163.0 0.0 copy-done.2
  163.1 0.0 copy-start.5
  163.1 5.5 %convolution_convert_fusion.refs_6_ = bf16[1120,1120]{1,0:T(8,128)(2,1)} fusion(bf16[1280,1120]{1,0:T(8,128)(2,1)S(1)} %get-tuple-element.107.refs_2_, bf16[1280,1120]{1,0:T(8,128)(2,1)S(1)} %copy-done.2), kind=kOutput, calls=%fused_computation.4 | convolution fusion | flops 3212518400 | bytes 8243200 | tf_op jit(solution)/shard_map/dot_general | solution.py:28
  168.5 0.0 copy-done.3
  168.5 0.0 copy-done.5
  168.5 9.1 %convert_reduce_fusion.1 = (f32[1120]{0:T(1024)S(1)}, bf16[1280,1120]{1,0:T(8,128)(2,1)S(1)}) fusion(f32[1280,1120]{1,0:T(8,128)S(1)} %get-tuple-element.108, bf16[1280,1120]{1,0:T(8,128)(2,1)S(1)} %copy-done.2, bf16[1120,1120]{1,0:T(8,128)(2,1)S(1)} %copy-done.5), kind=kOutput, calls=%fused_computation.13 | convolution fusion | flops 3241368576 | bytes 13982080 | tf_op jit(solution)/shard_map/dot_general | solution.py:24
  177.7 0.0 copy-start.4
  177.7 5.5 %convolution_convert_fusion.1.refs_5_ = bf16[1120,1120]{1,0:T(8,128)(2,1)} fusion(bf16[1280,1120]{1,0:T(8,128)(2,1)S(1)} %copy-done.15, bf16[1280,1120]{1,0:T(8,128)(2,1)S(1)} %get-tuple-element.110.refs_0_), kind=kOutput, calls=%fused_computation.5 | convolution fusion | flops 3212518400 | bytes 8243200 | tf_op jit(solution)/shard_map/dot_general | solution.py:28
  183.2 0.0 copy-done.4
  183.2 56.7 %back.1 = (f32[320,1120]{1,0:T(8,128)}, bf16[320,1120]{1,0:T(8,128)(2,1)}, f32[320,1120]{1,0:T(8,128)}, bf16[1280,1120]{1,0:T(8,128)(2,1)}, bf16[576,1120]{1,0:T(8,128)(2,1)}, /*index=5*/f32[8,1120]{1,0:T(8,128)}) custom-call(bf16[1280,1120]{1,0:T(8,128)(2,1)} %copy-done.4, bf16[1120,1120]{1,0:T(8,128)(2,1)} %get-tuple-element.69.refs_1_, ...), custom_call_target="tpu_custom_call" | custom-call | tf_op jit(solution)/shard_map/back/pallas_call | solution.py:1161
  239.9 2.9 collective-permute-start.3
  242.8 0.5 collective-permute-start.2
  243.4 0.8 slice.52
  244.1 24.6 %attn_bwd.1 = (bf16[1280,280]{1,0:T(8,128)(2,1)}, bf16[1280,280]{1,0:T(8,128)(2,1)}, bf16[1280,280]{1,0:T(8,128)(2,1)}) custom-call(s32[6]{0:T(128)} %pad_add_fusion.meta, s32[1,1408]{1,0:T(1,128)} %get-tuple-element.55.start, bf16[1280,384]{1,0:T(8,128)(2,1)} %get-tuple-element.74.qs, bf16[1280,384]{1,0:T(8,128)(2,1)} %get-tuple-element.75.ks, ...), custom_call_target="tpu_custom_call" | custom-call | flops 3670016000 | bytes 5734400 | tf_op jit(solution)/shard_map/attn_bwd/pallas_call | solution.py:265
  268.8 0.0 copy-done.11
  268.8 4.0 %convolution_convert_fusion.2.refs_13_ = bf16[280,1120]{1,0:T(8,128)(2,1)} fusion(bf16[1280,280]{1,0:T(8,128)(2,1)S(1)} %copy-done.11, bf16[1280,1120]{1,0:T(8,128)(2,1)} %get-tuple-element.77.gm), kind=kOutput, calls=%fused_computation.16 | convolution fusion | flops 803129600 | bytes 4211200 | tf_op jit(solution)/shard_map/dot_general | solution.py:28
  272.8 0.8 collective-permute-done.2.refs_1_
  273.6 0.2 convert_reduce_fusion.3
  273.8 2.0 convolution_convert_fusion.5.refs_10_
  275.8 0.0 collective-permute-done.3.refs_7_
  275.8 0.2 convert_reduce_fusion.2
  276.0 2.0 convolution_convert_fusion.3.refs_12_
  278.0 0.0 copy-done.10
  278.0 2.0 convolution_convert_fusion.4.refs_11_
  280.0 0.1 select_maximum_fusion
  280.0 0.1 broadcast_select_fusion
  280.1 1.3 concatenate.19.refs_14_
  281.4 85.9 %exit.1 = (bf16[320,1120]{1,0:T(8,128)(2,1)}, bf16[320,1120]{1,0:T(8,128)(2,1)}, bf16[1152,1120]{1,0:T(8,128)(2,1)}, bf16[1152,1120]{1,0:T(8,128)(2,1)}, bf16[1152,1120]{1,0:T(8,128)(2,1)}, /*index=5*/f32[16,1120]{1,0:T(8,128)}) custom-call(f32[320,1120]{1,0:T(8,128)} %get-tuple-element.72.refs_0_, bf16[320,1120]{1,0:T(8,128)(2,1)} %collective-permute-done.2.refs_1_, ...), custom_call_target="tpu_custom_call" | custom-call | tf_op jit(solution)/shard_map/exit/pallas_call | solution.py:1196
  367.3 0.0 copy-start.7
  367.3 3.8 %convert_bitcast_fusion = f32[3,1120,280]{1,2,0:T(8,128)} fusion(bf16[4,288,1120]{2,1,0:T(8,128)(2,1)} %bitcast.35), kind=kLoop, calls=%fused_computation.15 | loop fusion | flops 940800 | bytes 5644800 | tf_op jit(solution)/shard_map/transpose | solution.py:1337
  371.1 2.2 fusion.6
  373.3 2.7 slice_convert_fusion
  376.0 0.2 copy-done.6
  376.2 2.7 slice_convert_fusion.1
  378.9 1.7 slice_reduce_fusion
  380.6 0.7 dynamic-slice_reduce_fusion.1
  381.3 0.7 reshape_squeeze.3
  382.0 0.9 copy.39
  382.9 0.9 copy.40
  (25 shorter events, 0.1 us)
Async XLA Ops:
  0.6 4.4 %slice-start = ((bf16[1120,1120]{1,0:T(8,128)(2,1)}), bf16[32,1120]{1,0:T(8,128)(2,1)S(1)}, s32[]{:S(2)}) async-start(bf16[1120,1120]{1,0:T(8,128)(2,1)} %wu.1), calls=%async_computation | async-start | bytes 147456 | tf_op jit(solution)/shard_map/slice | solution.py:1242
  0.7 4.4 %slice-start.1 = ((bf16[1120,1120]{1,0:T(8,128)(2,1)}), bf16[32,1120]{1,0:T(8,128)(2,1)S(1)}, s32[]{:S(2)}) async-start(bf16[1120,1120]{1,0:T(8,128)(2,1)} %wd.1), calls=%async_computation.1 | async-start | bytes 147456 | tf_op jit(solution)/shard_map/slice | solution.py:1242
  74.3 34.2 %collective-permute-start = (bf16[608,1120]{1,0:T(8,128)(2,1)S(1)}, bf16[608,1120]{1,0:T(8,128)(2,1)S(1)}, u32[]{:S(2)}, u32[]{:S(2)}) collective-permute-start(bf16[608,1120]{1,0:T(8,128)(2,1)S(1)} %pad_maximum_fusion), channel_id=1, source_target_pairs={{0,2},{1,3},{6,4},{7,5},{8,10},{9,11},{14,12},{15,13},{16,18},{17,... | collective-permute-start | bytes 4085768 | tf_op jit(solution)/shard_map/ppermute | solution.py:1245
  75.6 24.5 %collective-permute-start.1 = (bf16[320,1120]{1,0:T(8,128)(2,1)}, bf16[320,1120]{1,0:T(8,128)(2,1)}, u32[]{:S(2)}, u32[]{:S(2)}) collective-permute-start(bf16[320,1120]{1,0:T(8,128)(2,1)} %get-tuple-element.65.cot_own), channel_id=1, source_target_pairs={{0,1},{1,0},{2,3},{3,2},{4,5},{5,4},{6,7},{7,6},{8,9},{9,8},{10,11... | collective-permute-start | bytes 2150408 | tf_op jit(solution)/shard_map/ppermute | solution.py:1244
  108.5 1.1 copy-start.8
  109.6 45.7 %copy-start.16 = (f32[1120]{0:T(1024)S(1)}, f32[1120]{0:T(1024)}, u32[]{:S(2)}) copy-start(f32[1120]{0:T(1024)} %get-tuple-element.70) | copy-start | bytes 13444
  155.3 7.7 %copy-start.2 = (bf16[1280,1120]{1,0:T(8,128)(2,1)S(1)}, bf16[1280,1120]{1,0:T(8,128)(2,1)}, u32[]{:S(2)}) copy-start(bf16[1280,1120]{1,0:T(8,128)(2,1)} %get-tuple-element.66.refs_7_) | copy-start | bytes 8601604
  163.0 5.5 %copy-start.3 = (bf16[1280,1120]{1,0:T(8,128)(2,1)}, bf16[1280,1120]{1,0:T(8,128)(2,1)S(1)}, u32[]{:S(2)}) copy-start(bf16[1280,1120]{1,0:T(8,128)(2,1)S(1)} %get-tuple-element.107.refs_2_) | copy-start | bytes 8601604
  163.1 5.5 %copy-start.5 = (bf16[1120,1120]{1,0:T(8,128)(2,1)S(1)}, bf16[1120,1120]{1,0:T(8,128)(2,1)}, u32[]{:S(2)}) copy-start(bf16[1120,1120]{1,0:T(8,128)(2,1)} %get-tuple-element.67.refs_3_) | copy-start | bytes 7526404
  168.5 9.2 %copy-start.15 = (bf16[1280,1120]{1,0:T(8,128)(2,1)S(1)}, bf16[1280,1120]{1,0:T(8,128)(2,1)}, u32[]{:S(2)}) copy-start(bf16[1280,1120]{1,0:T(8,128)(2,1)} %get-tuple-element.68) | copy-start | bytes 8601604
  177.7 5.5 %copy-start.4 = (bf16[1280,1120]{1,0:T(8,128)(2,1)}, bf16[1280,1120]{1,0:T(8,128)(2,1)S(1)}, u32[]{:S(2)}) copy-start(bf16[1280,1120]{1,0:T(8,128)(2,1)S(1)} %get-tuple-element.110.refs_0_) | copy-start | bytes 8601604
  239.9 35.8 %collective-permute-start.3 = (bf16[576,1120]{1,0:T(8,128)(2,1)}, bf16[576,1120]{1,0:T(8,128)(2,1)S(1)}, u32[]{:S(2)}, u32[]{:S(2)}) collective-permute-start(bf16[576,1120]{1,0:T(8,128)(2,1)} %get-tuple-element.82.refs_6_), channel_id=1, source_target_pairs={{2,0},{3,1},{4,6},{5,7},{10,8},{11,9},{12,14},{13,15},{18,16},{19,... | collective-permute-start | bytes 3870728 | tf_op jit(solution)/shard_map/ppermute | solution.py:1287
  242.8 30.7 %collective-permute-start.2 = (bf16[320,1120]{1,0:T(8,128)(2,1)}, bf16[320,1120]{1,0:T(8,128)(2,1)}, u32[]{:S(2)}, u32[]{:S(2)}) collective-permute-start(bf16[320,1120]{1,0:T(8,128)(2,1)} %get-tuple-element.73), channel_id=1, source_target_pairs={{0,1},{1,0},{2,3},{3,2},{4,5},{5,4},{6,7},{7,6},{8,9},{9,8},{10,11... | collective-permute-start | bytes 2150408 | tf_op jit(solution)/shard_map/ppermute | solution.py:1288
  244.1 24.6 %copy-start.11 = (bf16[1280,280]{1,0:T(8,128)(2,1)S(1)}, bf16[1280,280]{1,0:T(8,128)(2,1)}, u32[]{:S(2)}) copy-start(bf16[1280,280]{1,0:T(8,128)(2,1)} %get-tuple-element.61.att.o) | copy-start | bytes 2150404
  268.8 4.8 %copy-start = (bf16[1280,280]{1,0:T(8,128)(2,1)S(1)}, bf16[1280,280]{1,0:T(8,128)(2,1)}, u32[]{:S(2)}) copy-start(bf16[1280,280]{1,0:T(8,128)(2,1)} %get-tuple-element.81.refs_2_) | copy-start | bytes 2150404
  268.8 5.0 %copy-start.14 = (bf16[1280,1120]{1,0:T(8,128)(2,1)S(1)}, bf16[1280,1120]{1,0:T(8,128)(2,1)}, u32[]{:S(2)}) copy-start(bf16[1280,1120]{1,0:T(8,128)(2,1)} %get-tuple-element.58.normed) | copy-start | bytes 8601604
  273.8 2.0 copy-start.1
  275.8 2.2 copy-start.9
  276.0 2.0 copy-start.10
  367.3 6.1 %copy-start.7 = (bf16[1152,1120]{1,0:T(8,128)(2,1)S(1)}, bf16[1152,1120]{1,0:T(8,128)(2,1)}, u32[]{:S(2)}) copy-start(bf16[1152,1120]{1,0:T(8,128)(2,1)} %get-tuple-element.95) | copy-start | bytes 7741444
  373.3 2.9 copy-start.6
  376.2 5.8 %copy-start.13 = (bf16[320,1120]{1,0:T(8,128)(2,1)S(1)}, bf16[320,1120]{1,0:T(8,128)(2,1)}, u32[]{:S(2)}) copy-start(bf16[320,1120]{1,0:T(8,128)(2,1)} %get-tuple-element.90) | copy-start | bytes 2150404
  376.2 6.7 %copy-start.12 = (bf16[320,1120]{1,0:T(8,128)(2,1)S(1)}, bf16[320,1120]{1,0:T(8,128)(2,1)}, u32[]{:S(2)}) copy-start(bf16[320,1120]{1,0:T(8,128)(2,1)} %get-tuple-element.91) | copy-start | bytes 2150404
